TPU v7x, 32 devices: a whole 2x2x4 slice. The times are simulated.
32 devices in a mesh: face: 2 (over y), ty: 4 (over x, core), tx: 4 (over z).
Axes of the slice: x: 2, y: 2, z: 4, core: 2. Of those that a mesh axis runs over, the one named last changes fastest.
Arguments:
- cotangent: float32 [2, 32, 32, 128], P('face', 'ty', 'tx'), may hold values from -6 to 6
- courant_x: float32 [2, 32, 36, 32], P('face', 'ty', 'tx'), may hold values from -0.6 to 0.6
- edge_x: float32 [2, 32, 36], P('face', 'ty', 'tx'), may hold values from 0.7 to 1.4
- courant_y: float32 [2, 36, 32, 32], P('face', 'ty', 'tx'), may hold values from -0.6 to 0.6
- edge_y: float32 [2, 36, 32], P('face', 'ty', 'tx'), may hold values from 0.7 to 1.4
- cell_area: float32 [2, 32, 32], P('face', 'ty', 'tx'), may hold values from 0.7 to 1.4
- seam_partner: int32 [2, 4], replicated, may hold values from 0 to 7, as said below
- seam_flip: int32 [2, 4], replicated, may hold values from 0 to 1, as said below
Outputs:
- sensitivity: float32 [2, 32, 32, 128], P('face', 'ty', 'tx')
Inputs may be any that keep to these rules, and one draw needn't show every extreme that they name: `seam_partner`: the gluing pairs face edges: the partner of an edge's partner is that edge, and no edge is glued to itself; some east or west edge is glued to a north or south edge. `seam_flip`: the same for both edges of a glued pair.
All inputs are finite; a program needn't handle non-finite values.
Results may differ from a plain program's by a relative error of at most 0.0003.
Values sent between devices are 32-bit elements; how exact they have to be, the bound alone decides.
No kernel may reach another device: no remote copies, remote signals or barrier semaphores. Data moves between devices by JAX's collectives and lax.ppermute only.
A program may use at most 64 MiB of HBM per device.

v0:
```python
import jax
import jax.numpy as jnp
from jax import lax
from jax.sharding import PartitionSpec as P

STEPS = 2


def padded(cells, sides, width):
    for axis, dim in sides:
        count = lax.axis_size(axis)
        ends = count - 1
        head = lax.slice_in_dim(cells, 0, width, axis=dim)
        tail = lax.slice_in_dim(cells, cells.shape[dim] - width, cells.shape[dim], axis=dim)
        cells = jnp.concatenate(
            [
                lax.ppermute(tail, axis, [(i, (i + 1) % count) for i in range(ends)]),
                cells,
                lax.ppermute(head, axis, [((i + 1) % count, i) for i in range(ends)]),
            ],
            axis=dim,
        )
    return cells


def take_slab(source, axis_at, anchor, finish):
    return lax.slice_in_dim(source, anchor, finish, axis=axis_at)


def parabolic_sweep(extended, courant, edge_length, area_cells, axis_at):
    inner_count = extended.shape[axis_at] - 6
    interface_value = 7.0 / 12.0 * (
        take_slab(extended, axis_at, 1, inner_count + 4)
        + take_slab(extended, axis_at, 2, inner_count + 5)
    ) - 1.0 / 12.0 * (
        take_slab(extended, axis_at, 0, inner_count + 3)
        + take_slab(extended, axis_at, 3, inner_count + 6)
    )
    a_low = take_slab(interface_value, axis_at, 0, inner_count + 1)
    a_mid = take_slab(interface_value, axis_at, 1, inner_count + 2)
    a_high = take_slab(interface_value, axis_at, 2, inner_count + 3)
    left_cell = take_slab(extended, axis_at, 2, inner_count + 3)
    right_cell = take_slab(extended, axis_at, 3, inner_count + 4)
    curve_left = 6.0 * left_cell - 3.0 * (a_low + a_mid)
    curve_right = 6.0 * right_cell - 3.0 * (a_mid + a_high)
    upwind = -courant
    from_left = a_mid - 0.5 * courant * (a_mid - a_low - (1.0 - courant * (2.0 / 3.0)) * curve_left)
    from_right = a_mid + 0.5 * upwind * (
        a_high - a_mid + (1.0 - upwind * (2.0 / 3.0)) * curve_right
    )
    face_value = jnp.where(courant > 0, from_left, from_right)
    flux_term = courant * edge_length * face_value
    return (
        take_slab(extended, axis_at, 3, inner_count + 3)
        - (
            take_slab(flux_term, axis_at, 1, inner_count + 1)
            - take_slab(flux_term, axis_at, 0, inner_count)
        )
        / area_cells
    )


def indicator(flag):
    return flag.astype(jnp.float32)


def on_device(cotangent, courant_x, edge_x, courant_y, edge_y, cell_area, seam_partner, seam_flip):
    adjoint = cotangent[0]
    height_cells, width_cells, lanes_all = adjoint.shape
    repeat_count = lanes_all // courant_x.shape[-1]
    tiles_wide = lax.axis_size("tx")
    tiles_high = lax.axis_size("ty")
    face_index = lax.axis_index("face")
    row_index = lax.axis_index("ty")
    column_index = lax.axis_index("tx")
    spread_x = jnp.tile(courant_x[0], repeat_count)
    length_x = edge_x[0][:, :, None]
    spread_y = jnp.tile(courant_y[0], repeat_count)
    length_y = edge_y[0][:, :, None]
    area_cells = cell_area[0][:, :, None]
    own_codes = lax.dynamic_index_in_dim(seam_partner, face_index, 0, keepdims=False)
    own_flips = lax.dynamic_index_in_dim(seam_flip, face_index, 0, keepdims=False)
    on_east = indicator(column_index == tiles_wide - 1)
    on_west = indicator(column_index == 0)
    on_north = indicator(row_index == tiles_high - 1)
    on_south = indicator(row_index == 0)

    def deliver(strips, parity):
        gathered = lax.all_gather(strips[None], "face", axis=0, tiled=True)
        result = jnp.zeros((height_cells, width_cells, lanes_all), jnp.float32)
        for border in range(4):
            code = own_codes[border]
            other_face = code // 4
            other_border = code % 4
            active = indicator(other_border % 2 == parity)
            chosen = lax.dynamic_index_in_dim(gathered, other_face, 0, keepdims=False)
            chosen = lax.dynamic_index_in_dim(chosen, other_border // 2, 0, keepdims=False)
            chosen = jnp.where(own_flips[border] == 1, chosen[:, ::-1], chosen)
            if border == 0 or border == 2:
                segment = lax.dynamic_slice_in_dim(
                    chosen, row_index * height_cells, height_cells, 1
                )
                columns = jnp.swapaxes(segment, 0, 1)
                if border == 0:
                    result = result.at[:, width_cells - 3 :].add(
                        columns[:, ::-1] * (active * on_east)
                    )
                else:
                    result = result.at[:, :3].add(columns * (active * on_west))
            else:
                segment = lax.dynamic_slice_in_dim(
                    chosen, column_index * width_cells, width_cells, 1
                )
                if border == 1:
                    result = result.at[height_cells - 3 :].add(segment[::-1] * (active * on_north))
                else:
                    result = result.at[:3].add(segment * (active * on_south))
        return result

    def reverse_x(current):
        blank = jnp.zeros((height_cells, width_cells + 6, lanes_all), jnp.float32)

        def sweep_x(extended):
            return parabolic_sweep(extended, spread_x, length_x, area_cells, 1)

        unused, pullback = jax.vjp(sweep_x, blank)
        halo_adjoint = pullback(current)[0]
        own_part = halo_adjoint[:, 3 : width_cells + 3]
        west_rim = halo_adjoint[:, :3]
        east_rim = halo_adjoint[:, width_cells + 3 :]
        packed = jnp.concatenate([west_rim, east_rim], axis=1)
        bordered = padded(packed, (("tx", 1),), 3)
        own_part = (
            own_part.at[:, :3].add(bordered[:, :3]).at[:, width_cells - 3 :].add(bordered[:, 9:])
        )
        east_piece = jnp.swapaxes(east_rim, 0, 1) * on_east
        west_piece = jnp.swapaxes(west_rim[:, ::-1], 0, 1) * on_west
        pieces = jnp.stack([east_piece, west_piece])
        row_total = lax.psum(pieces, "tx")
        strips = lax.all_gather(row_total, "ty", axis=2, tiled=True)
        return own_part + deliver(strips, 0)

    def reverse_y(current):
        blank = jnp.zeros((height_cells + 6, width_cells, lanes_all), jnp.float32)

        def sweep_y(extended):
            return parabolic_sweep(extended, spread_y, length_y, area_cells, 0)

        unused, pullback = jax.vjp(sweep_y, blank)
        halo_adjoint = pullback(current)[0]
        own_part = halo_adjoint[3 : height_cells + 3]
        south_rim = halo_adjoint[:3]
        north_rim = halo_adjoint[height_cells + 3 :]
        packed = jnp.concatenate([south_rim, north_rim], axis=0)
        bordered = padded(packed, (("ty", 0),), 3)
        own_part = own_part.at[:3].add(bordered[:3]).at[height_cells - 3 :].add(bordered[9:])
        north_piece = north_rim * on_north
        south_piece = south_rim[::-1] * on_south
        pieces = jnp.stack([north_piece, south_piece])
        column_total = lax.psum(pieces, "ty")
        strips = lax.all_gather(column_total, "tx", axis=2, tiled=True)
        return own_part + deliver(strips, 1)

    for repeat in range(STEPS):
        adjoint = reverse_y(adjoint)
        adjoint = reverse_x(adjoint)
    return adjoint[None]


def solution(mesh):
    placed = (
        P("face", "ty", "tx", None),
        P("face", "ty", "tx", None),
        P("face", "ty", "tx"),
        P("face", "ty", "tx", None),
        P("face", "ty", "tx"),
        P("face", "ty", "tx"),
        P(),
        P(),
    )
    return jax.shard_map(
        on_device,
        mesh=mesh,
        in_specs=placed,
        out_specs=P("face", "ty", "tx", None),
        check_vma=False,
    )
```

profile of v0, /device:TPU:0, one launch (start us, length us, event | category | flops | bytes accessed | tf_op | source)
XLA Modules:
  0.0 164.9 jit_solution(16922162289223766744)
XLA Ops:
  0.0 0.8 copy.66
  0.8 0.8 tile.21
  1.6 0.0 copy-start
  1.6 0.1 tile.22
  1.7 0.6 copy-done
  2.3 0.1 fusion.68
  2.4 0.0 copy-start.2
  2.4 0.7 copy-done.2
  3.1 0.1 fusion.17
  3.3 0.1 pad_add_fusion.2
  3.4 2.4 %collective-permute-start = (f32[3,8,128]{2,0,1:T(4,128)S(1)}, f32[3,8,128]{2,0,1:T(4,128)S(1)}, u32[]{:S(2)}, u32[]{:S(2)}) collective-permute-start(f32[3,8,128]{2,0,1:T(4,128)S(1)} %get-tuple-element.367), channel_id=1, source_target_pairs={{0,4},{4,8},{8,12},{1,5},{5,9},{9,13},{2,6},{6,10},{10,14},{3,7},{... | collective-permute-start | bytes 36872 | tf_op jit(solution)/shard_map/ppermute | solution.py:17
  5.8 1.3 collective-permute-start.1
  7.1 0.0 copy-start.4
  7.1 0.0 copy-start.5
  7.1 0.7 copy-done.4
  7.8 0.0 copy-done.5
  7.8 0.7 fusion.70
  19.3 13.4 %psum.28 = f32[2,3,8,128]{3,1,2,0:T(4,128)S(1)} all-reduce(f32[2,3,8,128]{3,1,2,0:T(4,128)S(1)} %pad_maximum_fusion), channel_id=1, replica_groups=mesh['face'=2,'ty'=4,'tx'=4] {'ty'}, use_global_device_ids=true, to_apply=%region_0.1 | all-reduce | flops 6144 | bytes 49152 | tf_op jit(solution)/shard_map/psum | solution.py:160
  32.7 13.6 %all_gather.24 = f32[2,3,32,128]{3,1,2,0:T(4,128)S(1)} all-gather(f32[2,3,8,128]{3,1,2,0:T(4,128)S(1)} %psum.28), channel_id=1, replica_groups=mesh['face'=2,'ty'=4,'tx'=4] {'tx'}, dimensions={2}, use_global_device_ids=true | all-gather | bytes 122880 | tf_op jit(solution)/shard_map/all_gather | solution.py:161
  46.3 5.3 %all-gather = f32[4,3,32,128]{3,2,1,0:T(8,128)S(1)} all-gather(f32[2,3,32,128]{3,2,1,0:T(8,128)S(1)} %copy.69), channel_id=2, replica_groups=mesh['face'=2,'ty'=4,'tx'=4] {'face'}, dimensions={0}, use_global_device_ids=true | all-gather | bytes 294912 | tf_op jit(solution)/shard_map/all_gather | solution.py:89
  51.6 0.7 fusion.69
  55.2 0.1 scatter-add.85
  55.4 0.0 copy-start.1
  55.4 0.7 copy-done.1
  56.2 0.0 copy-start.3
  56.2 0.1 tile.25
  56.3 0.1 scatter-add.89
  56.5 0.4 copy-done.3
  56.9 0.1 copy.72
  57.0 0.0 collective-permute-done
  57.0 0.1 scatter-add.80
  57.1 0.0 collective-permute-done.1
  57.1 0.1 scatter-add.81
  57.3 0.1 fusion.67
  57.4 0.1 fusion.29
  57.5 3.5 %collective-permute-start.2 = (f32[8,3,128]{2,0,1:T(8,128)S(1)}, f32[8,3,128]{2,0,1:T(8,128)S(1)}, u32[]{:S(2)}, u32[]{:S(2)}) collective-permute-start(f32[8,3,128]{2,0,1:T(8,128)S(1)} %get-tuple-element.333), channel_id=1, source_target_pairs={{0,1},{1,2},{2,3},{4,5},{5,6},{6,7},{8,9},{9,10},{10,11},{12,13},{... | collective-permute-start | bytes 36872 | tf_op jit(solution)/shard_map/ppermute | solution.py:17
  61.1 1.3 collective-permute-start.3
  62.4 20.3 %psum.29 = f32[2,3,8,128]{3,2,1,0:T(8,128)S(1)} all-reduce(f32[2,3,8,128]{3,2,1,0:T(8,128)S(1)} %pad_maximum_fusion.2), channel_id=1, replica_groups=mesh['face'=2,'ty'=4,'tx'=4] {'tx'}, use_global_device_ids=true, to_apply=%region_1.2 | all-reduce | flops 6144 | bytes 49152 | tf_op jit(solution)/shard_map/psum | solution.py:139
  82.6 5.3 %all_gather.26 = f32[2,3,32,128]{3,2,1,0:T(8,128)S(1)} all-gather(f32[2,3,8,128]{3,2,1,0:T(8,128)S(1)} %psum.29), channel_id=1, replica_groups=mesh['face'=2,'ty'=4,'tx'=4] {'ty'}, dimensions={2}, use_global_device_ids=true | all-gather | bytes 122880 | tf_op jit(solution)/shard_map/all_gather | solution.py:140
  88.0 5.7 %all-gather.1 = f32[4,3,32,128]{3,2,1,0:T(8,128)S(1)} all-gather(f32[2,3,32,128]{3,2,1,0:T(8,128)S(1)} %all_gather.26), channel_id=3, replica_groups=mesh['face'=2,'ty'=4,'tx'=4] {'face'}, dimensions={0}, use_global_device_ids=true | all-gather | bytes 294912 | tf_op jit(solution)/shard_map/all_gather | solution.py:89
  94.0 0.1 scatter-add.95
  94.2 0.1 scatter-add.99
  94.4 0.1 fusion.66
  94.5 0.1 fusion.20
  94.6 0.1 pad_add_fusion
  94.7 1.3 collective-permute-start.5
  96.1 3.0 %collective-permute-start.4 = (f32[3,8,128]{2,0,1:T(4,128)S(1)}, f32[3,8,128]{2,0,1:T(4,128)S(1)}, u32[]{:S(2)}, u32[]{:S(2)}) collective-permute-start(f32[3,8,128]{2,0,1:T(4,128)S(1)} %get-tuple-element.364), channel_id=1, source_target_pairs={{0,4},{4,8},{8,12},{1,5},{5,9},{9,13},{2,6},{6,10},{10,14},{3,7},{... | collective-permute-start | bytes 36872 | tf_op jit(solution)/shard_map/ppermute | solution.py:17
  99.1 11.7 %psum.30 = f32[2,3,8,128]{3,1,2,0:T(4,128)S(1)} all-reduce(f32[2,3,8,128]{3,1,2,0:T(4,128)S(1)} %pad_maximum_fusion.1), channel_id=1, replica_groups=mesh['face'=2,'ty'=4,'tx'=4] {'ty'}, use_global_device_ids=true, to_apply=%region_2.3 | all-reduce | flops 6144 | bytes 49152 | tf_op jit(solution)/shard_map/psum | solution.py:160
  110.8 13.5 %all_gather.28 = f32[2,3,32,128]{3,1,2,0:T(4,128)S(1)} all-gather(f32[2,3,8,128]{3,1,2,0:T(4,128)S(1)} %psum.30), channel_id=1, replica_groups=mesh['face'=2,'ty'=4,'tx'=4] {'tx'}, dimensions={2}, use_global_device_ids=true | all-gather | bytes 122880 | tf_op jit(solution)/shard_map/all_gather | solution.py:161
  124.3 5.3 %all-gather.2 = f32[4,3,32,128]{3,2,1,0:T(8,128)S(1)} all-gather(f32[2,3,32,128]{3,2,1,0:T(8,128)S(1)} %copy.75), channel_id=4, replica_groups=mesh['face'=2,'ty'=4,'tx'=4] {'face'}, dimensions={0}, use_global_device_ids=true | all-gather | bytes 294912 | tf_op jit(solution)/shard_map/all_gather | solution.py:89
  129.9 0.1 scatter-add.105
  130.1 0.1 scatter-add.109
  130.3 0.1 scatter-add.100
  130.4 0.1 scatter-add.101
  130.6 0.1 fusion.65
  130.7 0.1 fusion.30
  130.9 1.3 collective-permute-start.7
  132.2 4.5 %collective-permute-start.6 = (f32[8,3,128]{2,0,1:T(8,128)S(1)}, f32[8,3,128]{2,0,1:T(8,128)S(1)}, u32[]{:S(2)}, u32[]{:S(2)}) collective-permute-start(f32[8,3,128]{2,0,1:T(8,128)S(1)} %get-tuple-element.321), channel_id=1, source_target_pairs={{0,1},{1,2},{2,3},{4,5},{5,6},{6,7},{8,9},{9,10},{10,11},{12,13},{... | collective-permute-start | bytes 36872 | tf_op jit(solution)/shard_map/ppermute | solution.py:17
  136.7 15.8 %psum.31 = f32[2,3,8,128]{3,2,1,0:T(8,128)S(1)} all-reduce(f32[2,3,8,128]{3,2,1,0:T(8,128)S(1)} %pad_maximum_fusion.3), channel_id=1, replica_groups=mesh['face'=2,'ty'=4,'tx'=4] {'tx'}, use_global_device_ids=true, to_apply=%region_3.4 | all-reduce | flops 6144 | bytes 49152 | tf_op jit(solution)/shard_map/psum | solution.py:139
  152.5 5.3 %all_gather.30 = f32[2,3,32,128]{3,2,1,0:T(8,128)S(1)} all-gather(f32[2,3,8,128]{3,2,1,0:T(8,128)S(1)} %psum.31), channel_id=1, replica_groups=mesh['face'=2,'ty'=4,'tx'=4] {'ty'}, dimensions={2}, use_global_device_ids=true | all-gather | bytes 122880 | tf_op jit(solution)/shard_map/all_gather | solution.py:140
  157.8 5.7 %all-gather.3 = f32[4,3,32,128]{3,2,1,0:T(8,128)S(1)} all-gather(f32[2,3,32,128]{3,2,1,0:T(8,128)S(1)} %all_gather.30), channel_id=5, replica_groups=mesh['face'=2,'ty'=4,'tx'=4] {'face'}, dimensions={0}, use_global_device_ids=true | all-gather | bytes 294912 | tf_op jit(solution)/shard_map/all_gather | solution.py:89
  163.8 0.1 scatter-add.115
  164.0 0.1 scatter-add.119
  164.2 0.6 copy.80
  (106 shorter events, 1.5 us)
Async XLA Ops:
  1.6 0.8 copy-start
  2.4 0.7 copy-start.2
  3.4 53.6 %collective-permute-start = (f32[3,8,128]{2,0,1:T(4,128)S(1)}, f32[3,8,128]{2,0,1:T(4,128)S(1)}, u32[]{:S(2)}, u32[]{:S(2)}) collective-permute-start(f32[3,8,128]{2,0,1:T(4,128)S(1)} %get-tuple-element.367), channel_id=1, source_target_pairs={{0,4},{4,8},{8,12},{1,5},{5,9},{9,13},{2,6},{6,10},{10,14},{3,7},{... | collective-permute-start | bytes 36872 | tf_op jit(solution)/shard_map/ppermute | solution.py:17
  5.8 51.4 %collective-permute-start.1 = (f32[3,8,128]{2,0,1:T(4,128)S(1)}, f32[3,8,128]{2,0,1:T(4,128)S(1)}, u32[]{:S(2)}, u32[]{:S(2)}) collective-permute-start(f32[3,8,128]{2,0,1:T(4,128)S(1)} %get-tuple-element.366), channel_id=1, source_target_pairs={{4,0},{8,4},{12,8},{5,1},{9,5},{13,9},{6,2},{10,6},{14,10},{7,3},{... | collective-permute-start | bytes 36872 | tf_op jit(solution)/shard_map/ppermute | solution.py:19
  7.1 0.7 copy-start.4
  7.1 0.7 copy-start.5
  55.4 0.8 copy-start.1
  56.2 0.7 copy-start.3
  57.5 36.8 %collective-permute-start.2 = (f32[8,3,128]{2,0,1:T(8,128)S(1)}, f32[8,3,128]{2,0,1:T(8,128)S(1)}, u32[]{:S(2)}, u32[]{:S(2)}) collective-permute-start(f32[8,3,128]{2,0,1:T(8,128)S(1)} %get-tuple-element.333), channel_id=1, source_target_pairs={{0,1},{1,2},{2,3},{4,5},{5,6},{6,7},{8,9},{9,10},{10,11},{12,13},{... | collective-permute-start | bytes 36872 | tf_op jit(solution)/shard_map/ppermute | solution.py:17
  61.1 33.3 %collective-permute-start.3 = (f32[8,3,128]{2,0,1:T(8,128)S(1)}, f32[8,3,128]{2,0,1:T(8,128)S(1)}, u32[]{:S(2)}, u32[]{:S(2)}) collective-permute-start(f32[8,3,128]{2,0,1:T(8,128)S(1)} %get-tuple-element.307), channel_id=1, source_target_pairs={{1,0},{2,1},{3,2},{5,4},{6,5},{7,6},{9,8},{10,9},{11,10},{13,12},{... | collective-permute-start | bytes 36872 | tf_op jit(solution)/shard_map/ppermute | solution.py:19
  94.7 35.7 %collective-permute-start.5 = (f32[3,8,128]{2,0,1:T(4,128)S(1)}, f32[3,8,128]{2,0,1:T(4,128)S(1)}, u32[]{:S(2)}, u32[]{:S(2)}) collective-permute-start(f32[3,8,128]{2,0,1:T(4,128)S(1)} %get-tuple-element.363), channel_id=1, source_target_pairs={{4,0},{8,4},{12,8},{5,1},{9,5},{13,9},{6,2},{10,6},{14,10},{7,3},{... | collective-permute-start | bytes 36872 | tf_op jit(solution)/shard_map/ppermute | solution.py:19
  96.1 34.2 %collective-permute-start.4 = (f32[3,8,128]{2,0,1:T(4,128)S(1)}, f32[3,8,128]{2,0,1:T(4,128)S(1)}, u32[]{:S(2)}, u32[]{:S(2)}) collective-permute-start(f32[3,8,128]{2,0,1:T(4,128)S(1)} %get-tuple-element.364), channel_id=1, source_target_pairs={{0,4},{4,8},{8,12},{1,5},{5,9},{9,13},{2,6},{6,10},{10,14},{3,7},{... | collective-permute-start | bytes 36872 | tf_op jit(solution)/shard_map/ppermute | solution.py:17
  130.9 33.4 %collective-permute-start.7 = (f32[8,3,128]{2,0,1:T(8,128)S(1)}, f32[8,3,128]{2,0,1:T(8,128)S(1)}, u32[]{:S(2)}, u32[]{:S(2)}) collective-permute-start(f32[8,3,128]{2,0,1:T(8,128)S(1)} %get-tuple-element.295), channel_id=1, source_target_pairs={{1,0},{2,1},{3,2},{5,4},{6,5},{7,6},{9,8},{10,9},{11,10},{13,12},{... | collective-permute-start | bytes 36872 | tf_op jit(solution)/shard_map/ppermute | solution.py:19
  132.2 32.0 %collective-permute-start.6 = (f32[8,3,128]{2,0,1:T(8,128)S(1)}, f32[8,3,128]{2,0,1:T(8,128)S(1)}, u32[]{:S(2)}, u32[]{:S(2)}) collective-permute-start(f32[8,3,128]{2,0,1:T(8,128)S(1)} %get-tuple-element.321), channel_id=1, source_target_pairs={{0,1},{1,2},{2,3},{4,5},{5,6},{6,7},{8,9},{9,10},{10,11},{12,13},{... | collective-permute-start | bytes 36872 | tf_op jit(solution)/shard_map/ppermute | solution.py:17
where the time goes:
time: 166 us; the launch traced here: 165 us
  blocking collectives  121 us (73%)
  starting transfers between devices  18.7 us (11%)
  between operations  14.5 us (9%)
  local copies, waits for them, and re-layouts  9.41 us (6%)
    psum x2, blocking collectives, reverse_x(): row_total = lax.psum(pieces, 'tx')  36 us
    all_gather x2, blocking collectives, reverse_y(): strips = lax.all_gather(column_total, 'tx', axis=2, tiled=True)  27.1 us
    psum x2, blocking collectives, reverse_y(): column_total = lax.psum(pieces, 'ty')  25.1 us
    all_gather x4, blocking collectives, deliver(): gathered = lax.all_gather(strips[None], 'face', axis=0, tiled=True)  22 us
    ppermute x4, starting transfers between devices, padded(): lax.ppermute(tail, axis, [(i, (i + 1) % count) for i in range(ends)])  13.5 us
    all_gather x2, blocking collectives, reverse_x(): strips = lax.all_gather(row_total, 'ty', axis=2, tiled=True)  10.6 us
    ppermute x4, starting transfers between devices, padded(): lax.ppermute(head, axis, [((i + 1) % count, i) for i in range(ends)])  5.17 us
  transfers between devices with their start and end apart: 8, of which 0 were waited for; matrix products, arithmetic and copies ran while one was open for 3% of the time, Pallas kernels for 0%

commit v1 on v0

v1 whole, which is shorter than its diff:
```python
import functools

import jax
import jax.numpy as jnp
from jax import lax
from jax.experimental import pallas as pl
from jax.experimental.pallas import tpu as pltpu
from jax.sharding import PartitionSpec as P

STEPS = 2
AXES = ("face", "ty", "tx")
PARTS = 4
PAD = 16
VMEM = pl.BlockSpec(memory_space=pltpu.VMEM)
SMEM = pl.BlockSpec(memory_space=pltpu.SMEM)


def loop(count, body):
    if count <= 8:
        for i in range(count):
            body(i)
    else:
        lax.fori_loop(0, count, lambda i, carry: (body(i), carry)[1], 0)


def split_parts(block, width, axis):
    return [lax.slice_in_dim(block, q * width, (q + 1) * width, axis=axis) for q in range(PARTS)]


def turned(block, rows):
    return jnp.concatenate(split_parts(block.T, rows, 0), axis=1)


def pack_kernel(cot_ref, qx_ref, qy_ref, send_ref):
    cy, cx, lanes = cot_ref.shape
    levels = lanes // PARTS
    width = 3 * cx * PARTS

    def body(y):
        rows = jnp.concatenate([cot_ref[y], qx_ref[y], qy_ref[y]], axis=0)
        send_ref[:, y, 0:width] = turned(rows, levels)

    loop(cy, body)


def unpack_kernel(recv_ref, out_ref):
    cy, cx, _ = out_ref.shape

    def body(y):
        out_ref[y] = turned(recv_ref[:, y, :], cx)

    loop(cy, body)


def stencil(coefs, side):
    c_low, f_low, c_high, f_high = (
        jnp.concatenate([part] * PARTS, axis=1) for part in split_parts(coefs, side, 1)
    )

    def interface(c, f):
        size = jnp.abs(c)
        half = 0.5 * size
        w = 3.0 * half * (1.0 - (2.0 / 3.0) * size)
        plus = c > 0
        centre = f * (1.0 - half - w)
        outer = f * (half - w)
        cell = f * (2.0 * w)
        zero = jnp.zeros_like(c)
        o_low, o_high = jnp.where(plus, outer, zero), jnp.where(plus, zero, outer)
        s_low, s_high = jnp.where(plus, cell, zero), jnp.where(plus, zero, cell)
        near, far = 7.0 / 12.0, 1.0 / 12.0
        return (
            -far * o_low,
            near * o_low - far * centre,
            near * (centre + o_low) - far * o_high + s_low,
            near * (centre + o_high) - far * o_low + s_high,
            near * o_high - far * centre,
            -far * o_high,
        )

    low, high = interface(c_low, f_low), interface(c_high, f_high)
    return (
        low[0],
        low[1] - high[0],
        low[2] - high[1],
        1.0 + low[3] - high[2],
        low[4] - high[3],
        low[5] - high[4],
        -high[5],
    )


def sphere_kernel(
    tiles_high, tiles_wide, partner_ref, flip_ref, recv_ref, out_ref, beta, acc, field, prod, rim, turned_rim
):
    faces, side, lanes = field.shape
    cy, cx = side // tiles_high, side // tiles_wide
    slots = prod.shape[0]

    def assemble(i):
        f, ty = i // tiles_high, i % tiles_high
        rows = slice(ty * cy, (ty + 1) * cy) if isinstance(i, int) else pl.ds(ty * cy, cy)
        tiles = [recv_ref[i * tiles_wide + tx] for tx in range(tiles_wide)]
        for j, target in enumerate((field.at[f], acc.at[0, f], acc.at[1, f])):
            target[rows, :] = jnp.concatenate(
                [
                    tile[:, (q * 3 + j) * cx : (q * 3 + j + 1) * cx]
                    for q in range(PARTS)
                    for tile in tiles
                ],
                axis=1,
            )

    loop(faces * tiles_high, assemble)

    def coefficients(f):
        for k, value in enumerate(stencil(turned(acc[0, f], side), side)):
            beta[0, k, f] = value
        for k, value in enumerate(stencil(acc[1, f], side)):
            beta[1, k, f] = value

    loop(faces, coefficients)
    prod[...] = jnp.zeros_like(prod)
    row_id = lax.broadcasted_iota(jnp.int32, (lanes, lanes), 0)
    column_id = lax.broadcasted_iota(jnp.int32, (lanes, lanes), 1)
    mirror = jnp.zeros((lanes, lanes), jnp.float32)
    for q in range(PARTS):
        inside = (row_id >= q * side) & (row_id < (q + 1) * side)
        mirror = jnp.where(inside & (row_id + column_id == (2 * q + 1) * side - 1), 1.0, mirror)

    def sweep(d):
        def apply(f):
            cells = field[f]
            here = prod.at[f % slots]
            total = None
            for k in range(7):
                here[k, PAD : PAD + side, :] = beta[d, k, f] * cells
            for k in range(7):
                start = PAD - 8 - (k - 3)
                term = here[k, start : start + side + 16, :]
                total = term if total is None else total + term
            acc[d, f] = total[8 : 8 + side]
            acc[1 - d, f] = jnp.zeros((side, lanes), jnp.float32)
            rim[f, 0:8, :] = total[side + 8 :]
            rim[f, 8:16, :] = total[0:8]

        loop(faces, apply)
        flat = rim[...].reshape(faces * 16, lanes)
        turned_rim[...] = jnp.dot(
            flat, mirror, precision=lax.Precision.HIGHEST, preferred_element_type=jnp.float32
        ).reshape(faces, 16, lanes)
        for f in range(faces):
            for low in range(2):
                edge = 4 * f + d + 2 * low
                code = partner_ref[edge]
                flipped = flip_ref[edge] == 1
                other = code // 4
                border = code % 4
                layout = border % 2
                for depth in range(3):
                    source = 15 - depth if low else depth
                    row = jnp.where(
                        flipped,
                        turned_rim[f, source : source + 1, :],
                        rim[f, source : source + 1, :],
                    )
                    target = pl.ds(jnp.where(border < 2, side - 1 - depth, depth), 1)
                    acc[layout, other, target, :] = acc[layout, other, target, :] + row

        def merge(f):
            field[f] = turned(acc[d, f], side) + acc[1 - d, f]

        loop(faces, merge)

    for step in range(STEPS):
        sweep(1)
        sweep(0)

    def hand_out(i):
        f, ty = i // tiles_high, i % tiles_high
        rows = slice(ty * cy, (ty + 1) * cy) if isinstance(i, int) else pl.ds(ty * cy, cy)
        block = field[f, rows, :]
        for tx in range(tiles_wide):
            out_ref[i * tiles_wide + tx] = jnp.concatenate(
                [part[:, tx * cx : (tx + 1) * cx] for part in split_parts(block, side, 1)], axis=1
            )

    loop(faces * tiles_high, hand_out)


def ratios(courant, length, area, axis):
    count = courant.shape[axis]
    out = []
    for start in (0, 1):
        c = lax.slice_in_dim(courant, start, start + count - 1, axis=axis)
        e = lax.slice_in_dim(length, start, start + count - 1, axis=axis)
        out += [c, c * (e / area)[:, :, None]]
    return jnp.concatenate(out, axis=-1)


def on_device(cotangent, courant_x, edge_x, courant_y, edge_y, cell_area, seam_partner, seam_flip):
    cells = cotangent[0]
    cy, cx, lanes = cells.shape
    levels = courant_x.shape[-1]
    faces, tiles_high, tiles_wide = (lax.axis_size(axis) for axis in AXES)
    devices = faces * tiles_high * tiles_wide
    side = cx * tiles_wide
    width = PARTS * side
    if lanes != PARTS * levels or devices % levels or side != cy * tiles_high:
        raise ValueError("unsupported sizes")
    f32 = jnp.float32

    send = pl.pallas_call(
        pack_kernel,
        out_shape=jax.ShapeDtypeStruct((levels, cy, -(-3 * PARTS * cx // 128) * 128), f32),
        in_specs=[VMEM] * 3,
        out_specs=VMEM,
        name="pack",
    )(
        cells,
        ratios(courant_x[0], edge_x[0], cell_area[0], 1),
        ratios(courant_y[0], edge_y[0], cell_area[0], 0),
    )
    if devices > levels:
        send = jnp.tile(send, (devices // levels, 1, 1))
    spheres = lax.all_to_all(send, AXES, 0, 0, tiled=True)
    result = pl.pallas_call(
        functools.partial(sphere_kernel, tiles_high, tiles_wide),
        out_shape=jax.ShapeDtypeStruct((devices, cy, PARTS * cx), f32),
        in_specs=[SMEM, SMEM, VMEM],
        out_specs=VMEM,
        scratch_shapes=[
            pltpu.VMEM((2, 7, faces, side, width), f32),
            pltpu.VMEM((2, faces, side, width), f32),
            pltpu.VMEM((faces, side, width), f32),
            pltpu.VMEM((min(faces, 2), 7, side + 2 * PAD, width), f32),
            pltpu.VMEM((faces, 16, width), f32),
            pltpu.VMEM((faces, 16, width), f32),
        ],
        name="sphere",
    )(seam_partner.reshape(-1), seam_flip.reshape(-1), spheres)
    back = lax.all_to_all(result, AXES, 0, 0, tiled=True)
    return pl.pallas_call(
        unpack_kernel,
        out_shape=jax.ShapeDtypeStruct((cy, cx, lanes), f32),
        in_specs=[VMEM],
        out_specs=VMEM,
        name="unpack",
    )(back[:levels])[None]


def solution(mesh):
    placed = (
        P("face", "ty", "tx", None),
        P("face", "ty", "tx", None),
        P("face", "ty", "tx"),
        P("face", "ty", "tx", None),
        P("face", "ty", "tx"),
        P("face", "ty", "tx"),
        P(),
        P(),
    )
    return jax.shard_map(
        on_device,
        mesh=mesh,
        in_specs=placed,
        out_specs=P("face", "ty", "tx", None),
        check_vma=False,
    )
```

time: 166 us -> 40.2 us (0.24)
  blocking collectives: 121 us -> 8.99 us
  between operations: 14.5 us -> 0.09 us
  starting transfers between devices: 18.7 us -> 7.33 us
  Pallas kernels: 0 us -> 7.34 us
  waiting for transfers between devices: 0.02 us -> 7.01 us
  local copies, waits for them, and re-layouts: 9.41 us -> 6.7 us
    psum x4 -> x0, blocking collectives: 61.1 us -> none  [the longest x2 36 us: reverse_x(): row_total = lax.psum(pieces, 'tx')]
    all_gather x8 -> x0, blocking collectives: 59.7 us -> none  [the longest x2 27.1 us: reverse_y(): strips = lax.all_gather(column_total, 'tx', axis=2, tiled=True)]
    ppermute x8 -> x0, starting transfers between devices: 18.7 us -> none  [the longest x4 13.5 us: padded(): lax.ppermute(tail, axis, [(i, (i + 1) % count) for i in range(ends)])]
    all_to_all x0 -> x1, blocking collectives: none -> 8.99 us  [on_device(): back = lax.all_to_all(result, AXES, 0, 0, tiled=True)]
    pallas_call x0 -> x3, Pallas kernels: none -> 7.34 us  [the longest x1 3.83 us: on_device(): pl.pallas_call(functools.partial(sphere_kernel, tiles_high, tiles_wide),...]
    all_to_all x0 -> x1, starting transfers between devices: none -> 7.33 us  [on_device(): spheres = lax.all_to_all(send, AXES, 0, 0, tiled=True)]
    all_to_all x0 -> x1, waiting for transfers between devices: none -> 7.01 us  [on_device(): spheres = lax.all_to_all(send, AXES, 0, 0, tiled=True)]
    unnamed x13 -> x17, local copies, waits for them, and re-layouts: 3.12 us -> 4.09 us
  transfers between devices with their start and end apart: 8 -> 1, of which waited for: 0 -> 1; matrix products, arithmetic and copies ran while one was open for 3% -> 3% of each run, Pallas kernels for 0% -> 0%
where the time goes in v1:
time: 40.2 us; the launch traced here: 39.8 us
  blocking collectives  8.99 us (22%)
  Pallas kernels  7.34 us (18%)
  starting transfers between devices  7.33 us (18%)
  waiting for transfers between devices  7.01 us (17%)
  local copies, waits for them, and re-layouts  6.7 us (17%)
  other arithmetic  2.31 us (6%)
    all_to_all x1, blocking collectives, on_device(): back = lax.all_to_all(result, AXES, 0, 0, tiled=True)  8.99 us
    all_to_all x1, starting transfers between devices, on_device(): spheres = lax.all_to_all(send, AXES, 0, 0, tiled=True)  7.33 us
    all_to_all x1, waiting for transfers between devices, on_device(): spheres = lax.all_to_all(send, AXES, 0, 0, tiled=True)  7.01 us
    unnamed x17, local copies, waits for them, and re-layouts  4.09 us
    pallas_call x1, Pallas kernels, on_device(): pl.pallas_call(functools.partial(sphere_kernel, tiles_high, tiles_wide),...  3.83 us
    pallas_call x1, Pallas kernels, on_device(): pl.pallas_call(pack_kernel, out_shape=jax.ShapeDtypeStruct((levels, cy, -...  1.77 us
    pallas_call x1, Pallas kernels, on_device(): pl.pallas_call(unpack_kernel, out_shape=jax.ShapeDtypeStruct((cy, cx, lan...  1.73 us
    concatenate x2, other arithmetic, ratios(): return jnp.concatenate(out, axis=-1)  1.41 us
  transfers between devices with their start and end apart: 1, of which 1 were waited for; matrix products, arithmetic and copies ran while one was open for 3% of the time, Pallas kernels for 0%

profile of v1, /device:TPU:0, one launch (start us, length us, event | category | flops | bytes accessed | tf_op | source)
XLA Modules:
  0.0 39.8 jit_solution(14078144716267357575)
XLA Ops:
  0.0 0.8 %fusion.1 = (f32[1,8,8]{1,2,0:T(8,128)S(1)}, f32[1,8,8]{1,2,0:T(8,128)S(1)}) fusion(f32[1,9,8]{1,2,0:T(8,128)} %param.12), kind=kLoop, calls=%fused_computation.14 | loop fusion | bytes 1024 | tf_op jit(solution)/shard_map/slice | solution.py:196
  0.8 0.1 copy.12
  0.9 0.1 copy.13
  1.0 0.0 copy-start.1
  1.0 0.8 %copy.15 = f32[1,8,9,32]{3,2,1,0:T(8,128)S(1)} copy(f32[1,8,9,32]{3,1,2,0:T(8,128)} %param.9) | data formatting | bytes 18432 | tf_op args[1]
  1.8 0.0 copy-done.1
  1.8 0.0 copy-start.2
  1.8 0.0 copy-start.3
  1.8 0.7 %copy-done.2 = f32[1,8,9]{2,1,0:T(8,128)S(1)} copy-done((f32[1,8,9]{2,1,0:T(8,128)S(1)}, f32[1,8,9]{2,1,0:T(8,128)}, u32[]{:S(2)}) %copy-start.2) | copy-done | bytes 312
  2.5 0.0 copy-done.3
  2.5 0.1 bitcast_divide_fusion.1
  2.5 0.1 broadcast_multiply_fusion.1
  2.7 0.7 %pad_maximum_fusion.qx_ref = f32[8,8,128]{2,1,0:T(8,128)} fusion(f32[8,8,32]{2,1,0:T(8,128)S(1)} %get-tuple-element.22, f32[8,8,32]{2,1,0:T(8,128)S(1)} %get-tuple-element.21, f32[8,8,32]{2,1,0:T(8,128)S(1)} %get-tuple-element.23, f32[8,8,32]{2,1,0:T(8,128)S(1)} %get-tuple-element.24), kind=kLoop, calls=%fused_computation.1 | loop fusion | flops 24576 | bytes 65536 | tf_op jit(solution)/shard_map/concatenate | solution.py:198
  3.4 0.7 %pad_maximum_fusion.1.qy_ref = f32[8,8,128]{2,1,0:T(8,128)} fusion(f32[8,8,32]{2,1,0:T(8,128)S(1)} %get-tuple-element.12, f32[8,8,32]{2,1,0:T(8,128)S(1)} %get-tuple-element.10, f32[8,8,32]{2,1,0:T(8,128)S(1)} %get-tuple-element.11, f32[8,8,32]{2,1,0:T(8,128)S(1)} %get-tuple-element.9), kind=kLoop, calls=%fused_computation.2 | loop fusion | flops 24576 | bytes 65536 | tf_op jit(solution)/shard_map/concatenate | solution.py:198
  4.1 1.8 %pack.1 = f32[32,8,128]{2,1,0:T(8,128)} custom-call(f32[8,8,128]{2,1,0:T(8,128)} %bitcast.24, f32[8,8,128]{2,1,0:T(8,128)} %pad_maximum_fusion.qx_ref, f32[8,8,128]{2,1,0:T(8,128)} %pad_maximum_fusion.1.qy_ref), custom_call_target="tpu_custom_call" | custom-call | tf_op jit(solution)/shard_map/pack/pallas_call | solution.py:213
  5.8 0.0 copy-start.4
  5.8 7.3 %all-to-all-start = ((f32[32,8,128]{2,1,0:T(8,128)}), f32[32,8,128]{2,1,0:T(8,128)S(1)}, u32[]{:S(2)}, u32[]{:S(2)}) async-start(f32[32,8,128]{2,1,0:T(8,128)} %pack.1), calls=%async_computation | async-start | bytes 262144 | tf_op jit(solution)/shard_map/all_to_all | solution.py:226
  13.2 0.0 copy-done.4
  13.2 0.0 copy-start.5
  13.2 0.6 %reshape.30.partner_ref = s32[8]{0:T(128)} reshape(s32[2,4]{1,0:T(2,128)S(1)} %copy-done.4) | data formatting | bytes 64 | tf_op jit(solution)/shard_map/reshape | solution.py:241
  13.8 0.1 copy-done.5
  13.9 0.7 %reshape.31.flip_ref = s32[8]{0:T(128)} reshape(s32[2,4]{1,0:T(2,128)S(1)} %copy-done.5) | data formatting | bytes 64 | tf_op jit(solution)/shard_map/reshape | solution.py:241
  14.5 7.0 %all-to-all-done.recv_ref = f32[32,8,128]{2,1,0:T(8,128)S(1)} async-done(((f32[32,8,128]{2,1,0:T(8,128)}), f32[32,8,128]{2,1,0:T(8,128)S(1)}, u32[]{:S(2)}, u32[]{:S(2)}) %all-to-all-start) | async-done | bytes 131104 | tf_op jit(solution)/shard_map/all_to_all | solution.py:226
  21.6 0.0 copy-start
  21.6 0.6 %copy-done = f32[32,8,128]{2,1,0:T(8,128)} copy-done((f32[32,8,128]{2,1,0:T(8,128)}, f32[32,8,128]{2,1,0:T(8,128)S(1)}, u32[]{:S(2)}) %copy-start) | copy-done | bytes 131096
  22.2 3.8 %sphere.1 = f32[32,8,32]{2,1,0:T(8,128)} custom-call(s32[8]{0:T(128)} %reshape.30.partner_ref, s32[8]{0:T(128)} %reshape.31.flip_ref, f32[32,8,128]{2,1,0:T(8,128)} %copy-done), custom_call_target="tpu_custom_call" | custom-call | tf_op jit(solution)/shard_map/sphere/pallas_call | solution.py:227
  26.0 1.0 %reshape.32 = f32[32,1,256]{2,1,0:T(1,128)S(1)} reshape(f32[32,8,32]{2,1,0:T(8,128)} %sphere.1) | data formatting | bytes 65536
  27.1 9.0 %all_to_all.10 = f32[32,1,256]{2,1,0:T(1,128)S(1)} all-to-all(f32[32,1,256]{2,1,0:T(1,128)S(1)} %reshape.32), channel_id=1, replica_groups=mesh['face'=2,'ty'=4,'tx'=4] {'face','ty','tx'}, dimensions={0} | all-to-all | bytes 65536 | tf_op jit(solution)/shard_map/all_to_all | solution.py:242
  36.1 0.5 %broadcast.2 = f32[]{:T(128)} broadcast(f32[]{:T(128)} %constant.12), dimensions={} | broadcast | bytes 8 | tf_op jit(solution)/shard_map/all_to_all | solution.py:242
  36.6 0.7 %reduce = f32[32,256]{1,0:T(8,128)S(1)} reduce(f32[32,1,256]{2,1,0:T(1,128)S(1)} %all_to_all.10, f32[]{:T(128)} %broadcast.2), dimensions={1}, to_apply=%all_to_all.7.reduce_sub_computation | reduce | bytes 65540 | tf_op jit(solution)/shard_map/all_to_all | solution.py:242
  37.3 0.7 %reshape.33.recv_ref = f32[32,8,32]{2,1,0:T(8,128)} reshape(f32[32,256]{1,0:T(8,128)S(1)} %reduce) | data formatting | bytes 65536
  38.0 1.7 %unpack.1 = f32[8,8,128]{2,1,0:T(8,128)} custom-call(f32[32,8,32]{2,1,0:T(8,128)} %reshape.33.recv_ref), custom_call_target="tpu_custom_call" | custom-call | tf_op jit(solution)/shard_map/unpack/pallas_call | solution.py:243
  (1 shorter events, 0.0 us)
Async XLA Ops:
  1.0 0.8 %copy-start.1 = (f32[1,9,8,32]{3,2,1,0:T(8,128)S(1)}, f32[1,9,8,32]{3,2,1,0:T(8,128)}, u32[]{:S(2)}) copy-start(f32[1,9,8,32]{3,2,1,0:T(8,128)} %param.11) | copy-start | bytes 27652
  1.8 0.7 %copy-start.2 = (f32[1,8,9]{2,1,0:T(8,128)S(1)}, f32[1,8,9]{2,1,0:T(8,128)}, u32[]{:S(2)}) copy-start(f32[1,8,9]{2,1,0:T(8,128)} %param.10) | copy-start | bytes 868
  1.8 0.7 %copy-start.3 = (f32[1,8,8]{2,1,0:T(8,128)S(1)}, f32[1,8,8]{2,1,0:T(8,128)}, u32[]{:S(2)}) copy-start(f32[1,8,8]{2,1,0:T(8,128)} %param.13) | copy-start | bytes 772
  5.8 7.3 %copy-start.4 = (s32[2,4]{1,0:T(2,128)S(1)}, s32[2,4]{1,0:T(2,128)}, u32[]{:S(2)}) copy-start(s32[2,4]{1,0:T(2,128)} %param.14) | copy-start | bytes 100
  5.8 15.7 %all-to-all-start = ((f32[32,8,128]{2,1,0:T(8,128)}), f32[32,8,128]{2,1,0:T(8,128)S(1)}, u32[]{:S(2)}, u32[]{:S(2)}) async-start(f32[32,8,128]{2,1,0:T(8,128)} %pack.1), calls=%async_computation | async-start | bytes 262144 | tf_op jit(solution)/shard_map/all_to_all | solution.py:226
  13.2 0.7 %copy-start.5 = (s32[2,4]{1,0:T(2,128)S(1)}, s32[2,4]{1,0:T(2,128)}, u32[]{:S(2)}) copy-start(s32[2,4]{1,0:T(2,128)} %param.15) | copy-start | bytes 100
  21.6 0.6 %copy-start = (f32[32,8,128]{2,1,0:T(8,128)}, f32[32,8,128]{2,1,0:T(8,128)S(1)}, u32[]{:S(2)}) copy-start(f32[32,8,128]{2,1,0:T(8,128)S(1)} %all-to-all-done.recv_ref) | copy-start | bytes 393220

commit v2 on v1

v2 whole, which is shorter than its diff:
```python
import functools

import jax
import jax.numpy as jnp
from jax import lax
from jax.experimental import pallas as pl
from jax.experimental.pallas import tpu as pltpu
from jax.sharding import PartitionSpec as P

STEPS = 2
AXES = ("face", "ty", "tx")
PARTS = 4
PAD = 16
VMEM = pl.BlockSpec(memory_space=pltpu.VMEM)
SMEM = pl.BlockSpec(memory_space=pltpu.SMEM)


def loop(count, body):
    if count <= 8:
        for i in range(count):
            body(i)
    else:
        lax.fori_loop(0, count, lambda i, carry: (body(i), carry)[1], 0)


def split_parts(block, width, axis):
    return [lax.slice_in_dim(block, q * width, (q + 1) * width, axis=axis) for q in range(PARTS)]


def turned(block, rows):
    return jnp.concatenate(split_parts(block.T, rows, 0), axis=1)


def pack_kernel(cot_ref, cx_ref, ex_ref, cy_ref, ey_ref, area_ref, send_ref, rows_ref):
    cy, cx, lanes = cot_ref.shape
    levels = lanes // PARTS
    group = rows_ref.shape[1] // cx
    place = [
        pl.ds(pl.multiple_of((lax.axis_index("tx") + j) % group * cx, cx), cx) for j in range(3)
    ]
    area = area_ref[...]
    scale_x = [ex_ref[:, i : i + cx] / area for i in range(2)]
    scale_y = [ey_ref[:, i : i + cy] / area.T for i in range(2)]
    if group > 3:
        rows_ref[...] = jnp.zeros_like(rows_ref)

    by_x = []
    for x in range(cx):
        pieces = []
        for i in range(2):
            c = cx_ref[x + i]
            pieces += [c, c * scale_x[i][:, x : x + 1]]
        by_x.append(jnp.concatenate(pieces, axis=1))
    by_x = jnp.stack(by_x)
    for y0 in range(0, cy, 8):
        rows_ref[y0 : y0 + 8, place[1], :] = jnp.swapaxes(by_x[:, y0 : y0 + 8], 0, 1)
    for y in range(cy):
        pieces = []
        for i in range(2):
            c = cy_ref[y + i]
            pieces += [c, c * scale_y[i][:, y : y + 1]]
        rows_ref[y, place[2], :] = jnp.concatenate(pieces, axis=1)
        rows_ref[y, place[0], :] = cot_ref[y]
    for y in range(cy):
        send_ref[:, y, :] = turned(rows_ref[y], levels)


def unpack_kernel(recv_ref, out_ref, rows_ref):
    cy, cx, _ = out_ref.shape
    group = rows_ref.shape[1] // (PARTS * cx)
    place = lax.axis_index("tx") % group
    for y in range(cy):
        rows_ref[y] = recv_ref[:, y, :].T
        out_ref[y] = jnp.concatenate(
            [
                rows_ref[y, pl.ds(pl.multiple_of((q * group + place) * cx, cx), cx), :]
                for q in range(PARTS)
            ],
            axis=1,
        )


def stencil(coefs, side):
    c_low, f_low, c_high, f_high = (
        jnp.concatenate([part] * PARTS, axis=1) for part in split_parts(coefs, side, 1)
    )

    def interface(c, f):
        size = jnp.abs(c)
        half = 0.5 * size
        w = 3.0 * half * (1.0 - (2.0 / 3.0) * size)
        plus = c > 0
        centre = f * (1.0 - half - w)
        outer = f * (half - w)
        cell = f * (2.0 * w)
        zero = jnp.zeros_like(c)
        o_low, o_high = jnp.where(plus, outer, zero), jnp.where(plus, zero, outer)
        s_low, s_high = jnp.where(plus, cell, zero), jnp.where(plus, zero, cell)
        near, far = 7.0 / 12.0, 1.0 / 12.0
        return (
            -far * o_low,
            near * o_low - far * centre,
            near * (centre + o_low) - far * o_high + s_low,
            near * (centre + o_high) - far * o_low + s_high,
            near * o_high - far * centre,
            -far * o_high,
        )

    low, high = interface(c_low, f_low), interface(c_high, f_high)
    return (
        low[0],
        low[1] - high[0],
        low[2] - high[1],
        1.0 + low[3] - high[2],
        low[4] - high[3],
        low[5] - high[4],
        -high[5],
    )


def sphere_kernel(
    tiles_high, tiles_wide, partner_ref, flip_ref, recv_ref, out_ref, beta, acc, field, prod, rim
):
    faces, side, lanes = field.shape
    cy, cx = side // tiles_high, side // tiles_wide
    slots = prod.shape[0]
    slot_lanes = recv_ref.shape[2]
    group = slot_lanes // (PARTS * cx)
    span = group * cx
    lane_id = lax.broadcasted_iota(jnp.int32, (cy, slot_lanes), 1)
    place_id = lane_id // cx % group

    def row_block(i):
        f, ty = i // tiles_high, i % tiles_high
        start = ty * cy
        return f, pl.ds(start if isinstance(i, int) else pl.multiple_of(start, 8), cy)

    def assemble(i):
        f, rows = row_block(i)
        for j, target in enumerate((field, acc.at[0], acc.at[1])):
            blocks = []
            for first in range(0, tiles_wide, group):
                tiles = [recv_ref[i * tiles_wide + first + tx] for tx in range(group)]
                block = tiles[0]
                for tx in range(1, group):
                    block = jnp.where(place_id == (tx + j) % group, tiles[tx], block)
                if j:
                    ahead = pltpu.roll(block, slot_lanes - j * cx, 1)
                    around = pltpu.roll(block, span - j * cx, 1)
                    block = jnp.where(place_id < group - j, ahead, around)
                blocks.append(block)
            if len(blocks) == 1:
                value = blocks[0]
            else:
                value = jnp.concatenate(
                    [block[:, q * span : (q + 1) * span] for q in range(PARTS) for block in blocks],
                    axis=1,
                )
            target[f, rows, :] = value

    loop(faces * tiles_high, assemble)

    def coefficients(f):
        for k, value in enumerate(stencil(turned(acc[0, f], side), side)):
            beta[0, k, f] = value
        for k, value in enumerate(stencil(acc[1, f], side)):
            beta[1, k, f] = value

    loop(faces, coefficients)
    prod[...] = jnp.zeros_like(prod)
    rim[...] = jnp.zeros_like(rim)
    mirror_id = lax.broadcasted_iota(jnp.int32, (8, 128), 1)
    mirror_id = mirror_id // side * side + (side - 1 - mirror_id % side)

    def sweep(d):
        def apply(f):
            cells = field[f]
            here = prod.at[f % slots]
            total = None
            for k in range(7):
                here[k, PAD : PAD + side, :] = beta[d, k, f] * cells
            for k in range(7):
                start = PAD - 8 - (k - 3)
                term = here[k, start : start + side + 16, :]
                total = term if total is None else total + term
            acc[d, f] = total[8 : 8 + side]
            acc[1 - d, f] = jnp.zeros((side, lanes), jnp.float32)
            for low in range(2):
                rows = total[0:8] if low else total[side + 8 :]
                rim[0, low, f, low] = rows
                for depth in range(3):
                    source, target = (7 - depth, depth) if low else (depth, 7 - depth)
                    rim[0, 1 - low, f, low, target : target + 1, :] = rows[source : source + 1]
                for order in range(2):
                    value = rim[0, order, f, low]
                    rim[1, order, f, low] = jnp.concatenate(
                        [
                            jnp.take_along_axis(value[:, at : at + 128], mirror_id, axis=1)
                            for at in range(0, lanes, 128)
                        ],
                        axis=1,
                    )

        loop(faces, apply)
        for f in range(faces):
            for low in range(2):
                edge = d + 2 * low
                code = partner_ref[f, edge]
                other, border = code // 4, code % 4
                high = jnp.where(border < 2, 1, 0)
                rows = pl.ds(pl.multiple_of(high * (side - 8), 8), 8)
                layout = border % 2
                acc[layout, other, rows, :] = (
                    acc[layout, other, rows, :] + rim[flip_ref[f, edge], high, f, low]
                )

        def merge(f):
            field[f] = turned(acc[d, f], side) + acc[1 - d, f]

        loop(faces, merge)

    for step in range(STEPS):
        sweep(1)
        sweep(0)

    def hand_out(i):
        f, rows = row_block(i)
        block = field[f, rows, :]
        for first in range(0, tiles_wide, group):
            if group == tiles_wide:
                value = block
            else:
                value = jnp.concatenate(
                    [part[:, first * cx : first * cx + span] for part in split_parts(block, side, 1)],
                    axis=1,
                )
            for tx in range(first, first + group):
                out_ref[i * tiles_wide + tx] = value

    loop(faces * tiles_high, hand_out)


def grant(*blocks):
    words = sum(functools.reduce(lambda a, b: a * b, (*shape[:-2], -(-shape[-2] // 8) * 8, -(-shape[-1] // 128) * 128)) for shape in blocks)
    return pltpu.CompilerParams(vmem_limit_bytes=5 * words + (2 << 20))


def on_device(cotangent, courant_x, edge_x, courant_y, edge_y, cell_area, seam_partner, seam_flip):
    cells = cotangent[0]
    cy, cx, lanes = cells.shape
    levels = courant_x.shape[-1]
    faces, tiles_high, tiles_wide = (lax.axis_size(axis) for axis in AXES)
    devices = faces * tiles_high * tiles_wide
    side = cx * tiles_wide
    width = PARTS * side
    group = 128 // (PARTS * cx)
    if lanes != PARTS * levels or devices % levels or side != cy * tiles_high:
        raise ValueError("unsupported sizes")
    if cx % 8 or cy % 8 or group < 3 or tiles_wide % group or 128 % side:
        raise ValueError("unsupported tile")
    f32 = jnp.float32
    slot = PARTS * group * cx

    pack_rows = (cy, group * cx, lanes)
    send = pl.pallas_call(
        pack_kernel,
        out_shape=jax.ShapeDtypeStruct((levels, cy, slot), f32),
        in_specs=[VMEM] * 6,
        out_specs=VMEM,
        scratch_shapes=[pltpu.VMEM(pack_rows, f32)],
        compiler_params=grant(*[cells.shape] * 4, pack_rows, (levels, cy, slot)),
        name="pack",
    )(
        cells,
        jnp.swapaxes(courant_x[0], 0, 1),
        edge_x[0],
        courant_y[0],
        jnp.swapaxes(edge_y[0], 0, 1),
        cell_area[0],
    )
    if devices > levels:
        send = jnp.tile(send, (devices // levels, 1, 1))
    spheres = lax.all_to_all(send, AXES, 0, 0, tiled=True)
    scratch = [
        (2, 7, faces, side, width),
        (2, faces, side, width),
        (faces, side, width),
        (min(faces, 2), 7, side + 2 * PAD, width),
        (2, 2, faces, 2, 8, width),
    ]
    result = pl.pallas_call(
        functools.partial(sphere_kernel, tiles_high, tiles_wide),
        out_shape=jax.ShapeDtypeStruct((devices, cy, slot), f32),
        in_specs=[SMEM, SMEM, VMEM],
        out_specs=VMEM,
        scratch_shapes=[pltpu.VMEM(shape, f32) for shape in scratch],
        compiler_params=grant(*[(devices, cy, slot)] * 2, *scratch),
        name="sphere",
    )(seam_partner, seam_flip, spheres)
    back = lax.all_to_all(result, AXES, 0, 0, tiled=True)[:levels]
    unpack_rows = (cy, slot, levels)
    return pl.pallas_call(
        unpack_kernel,
        out_shape=jax.ShapeDtypeStruct((cy, cx, lanes), f32),
        in_specs=[VMEM],
        out_specs=VMEM,
        scratch_shapes=[pltpu.VMEM(unpack_rows, f32)],
        compiler_params=grant(cells.shape, back.shape, unpack_rows),
        name="unpack",
    )(back)[None]


def solution(mesh):
    placed = (
        P("face", "ty", "tx", None),
        P("face", "ty", "tx", None),
        P("face", "ty", "tx"),
        P("face", "ty", "tx", None),
        P("face", "ty", "tx"),
        P("face", "ty", "tx"),
        P(),
        P(),
    )
    return jax.shard_map(
        on_device,
        mesh=mesh,
        in_specs=placed,
        out_specs=P("face", "ty", "tx", None),
        check_vma=False,
    )
```

time: 40.2 us -> 33.4 us (0.83)
  blocking collectives: 8.99 us -> 25.6 us
  starting transfers between devices: 7.33 us -> 0 us
  waiting for transfers between devices: 7.01 us -> 0 us
  Pallas kernels: 7.34 us -> 3.67 us
  local copies, waits for them, and re-layouts: 6.7 us -> 3.69 us
  other arithmetic: 2.31 us -> 0 us
    all_to_all x1 -> x2, blocking collectives: 8.99 us -> 25.6 us  [the longest x1 15.5 us: on_device(): spheres = lax.all_to_all(send, AXES, 0, 0, tiled=True)]
    all_to_all x1 -> x0, starting transfers between devices: 7.33 us -> none  [on_device(): spheres = lax.all_to_all(send, AXES, 0, 0, tiled=True)]
    all_to_all x1 -> x0, waiting for transfers between devices: 7.01 us -> none  [on_device(): spheres = lax.all_to_all(send, AXES, 0, 0, tiled=True)]
    pallas_call x1, Pallas kernels: 3.83 us -> 2 us  [on_device(): pl.pallas_call(functools.partial(sphere_kernel, tiles_high, tiles_wide),...]
    concatenate x2 -> x0, other arithmetic: 1.41 us -> none  [ratios(): return jnp.concatenate(out, axis=-1)]
    reshape x2 -> x0, local copies, waits for them, and re-layouts: 1.26 us -> none  [the longest x1 0.67 us: on_device(): seam_flip.reshape(-1)]
    pallas_call x1, Pallas kernels: 1.77 us -> 0.63 us  [on_device(): pl.pallas_call(pack_kernel, out_shape=jax.ShapeDtypeStruct((levels, cy, s...]
    slice x2 -> x0, local copies, waits for them, and re-layouts: 0.84 us -> none  [the longest x1 0.83 us: ratios(): e = lax.slice_in_dim(length, start, start + count - 1, axis=axis)]
  transfers between devices with their start and end apart: 1 -> 0, of which waited for: 1 -> 0; matrix products, arithmetic and copies ran while one was open for 3% -> 0% of each run, Pallas kernels for 0% -> 0%
where the time goes in v2:
time: 33.4 us; the launch traced here: 33 us
  blocking collectives  25.6 us (77%)
  local copies, waits for them, and re-layouts  3.69 us (11%)
  Pallas kernels  3.67 us (11%)
    all_to_all x1, blocking collectives, on_device(): spheres = lax.all_to_all(send, AXES, 0, 0, tiled=True)  15.5 us
    all_to_all x1, blocking collectives, on_device(): back = lax.all_to_all(result, AXES, 0, 0, tiled=True)[:levels]  10.1 us
    unnamed x16, local copies, waits for them, and re-layouts  3.69 us
    pallas_call x1, Pallas kernels, on_device(): pl.pallas_call(functools.partial(sphere_kernel, tiles_high, tiles_wide),...  2 us
    pallas_call x1, Pallas kernels, on_device(): pl.pallas_call(unpack_kernel, out_shape=jax.ShapeDtypeStruct((cy, cx, lan...  1.03 us

profile of v2, /device:TPU:0, one launch (start us, length us, event | category | flops | bytes accessed | tf_op | source)
XLA Modules:
  0.0 33.0 jit_solution(3531005879415523726)
XLA Ops:
  0.0 0.0 copy-start.4
  0.0 0.0 copy-start.3
  0.0 0.7 %copy-done.4 = f32[1,9,8]{1,2,0:T(8,128)S(1)} copy-done((f32[1,9,8]{1,2,0:T(8,128)S(1)}, f32[1,9,8]{1,2,0:T(8,128)}, u32[]{:S(2)}) %copy-start.4) | copy-done | bytes 312
  0.7 0.0 copy-done.3
  0.7 0.0 copy-start
  0.7 0.8 %copy-done = f32[1,8,9,32]{3,1,2,0:T(8,128)S(1)} copy-done((f32[1,8,9,32]{3,1,2,0:T(8,128)S(1)}, f32[1,8,9,32]{3,1,2,0:T(8,128)}, u32[]{:S(2)}) %copy-start) | copy-done | bytes 9240
  1.5 0.0 copy-start.1
  1.5 0.8 %copy-done.1 = f32[1,9,8,32]{3,2,1,0:T(8,128)S(1)} copy-done((f32[1,9,8,32]{3,2,1,0:T(8,128)S(1)}, f32[1,9,8,32]{3,2,1,0:T(8,128)}, u32[]{:S(2)}) %copy-start.1) | copy-done | bytes 9240
  2.2 0.0 copy-start.2
  2.2 0.8 %copy-done.2 = f32[1,8,8,128]{3,2,1,0:T(8,128)S(1)} copy-done((f32[1,8,8,128]{3,2,1,0:T(8,128)S(1)}, f32[1,8,8,128]{3,2,1,0:T(8,128)}, u32[]{:S(2)}) %copy-start.2) | copy-done | bytes 32792
  3.0 0.0 copy-start.5
  3.0 0.7 %copy-done.5 = f32[1,8,8]{2,1,0:T(8,128)S(1)} copy-done((f32[1,8,8]{2,1,0:T(8,128)S(1)}, f32[1,8,8]{2,1,0:T(8,128)}, u32[]{:S(2)}) %copy-start.5) | copy-done | bytes 280
  3.7 0.6 %pack.1 = f32[32,8,128]{2,1,0:T(8,128)S(1)} custom-call(f32[8,8,128]{2,1,0:T(8,128)S(1)} %bitcast.13, f32[9,8,32]{2,1,0:T(8,128)S(1)} %bitcast.11, f32[8,9]{1,0:T(8,128)S(1)} %bitcast.14, f32[9,8,32]{2,1,0:T(8,128)S(1)} %bitcast.12, f32[8,9]{1,0:T(8,128)S(1)} %bitcast.15, f32[8,8]{1,0:T(8,128)S(1)} %bitcast.16), custom_call_target="tpu_custom_call" | custom-call | tf_op jit(solution)/shard_map/pack/pallas_call | solution.py:265
  4.3 0.0 copy-start.6
  4.3 0.0 copy-start.7
  4.4 15.5 %all_to_all.10.recv_ref = f32[32,8,128]{2,1,0:T(8,128)S(1)} all-to-all(f32[32,8,128]{2,1,0:T(8,128)S(1)} %pack.1), channel_id=1, replica_groups=mesh['face'=2,'ty'=4,'tx'=4] {'face','ty','tx'}, dimensions={0} | all-to-all | bytes 262144 | tf_op jit(solution)/shard_map/all_to_all | solution.py:283
  19.9 0.0 copy-done.6
  19.9 0.0 copy-done.7
  19.9 2.0 %sphere.1 = f32[32,8,128]{2,1,0:T(8,128)S(1)} custom-call(s32[2,4]{1,0:T(2,128)S(1)} %copy-done.6, s32[2,4]{1,0:T(2,128)S(1)} %copy-done.7, f32[32,8,128]{2,1,0:T(8,128)S(1)} %all_to_all.10.recv_ref), custom_call_target="tpu_custom_call" | custom-call | tf_op jit(solution)/shard_map/sphere/pallas_call | solution.py:291
  21.9 10.1 %all_to_all.11.recv_ref = f32[32,8,128]{2,1,0:T(8,128)S(1)} all-to-all(f32[32,8,128]{2,1,0:T(8,128)S(1)} %sphere.1), channel_id=1, replica_groups=mesh['face'=2,'ty'=4,'tx'=4] {'face','ty','tx'}, dimensions={0} | all-to-all | bytes 262144 | tf_op jit(solution)/shard_map/all_to_all | solution.py:300
  32.0 1.0 %unpack.1 = f32[8,8,128]{2,1,0:T(8,128)} custom-call(f32[32,8,128]{2,1,0:T(8,128)S(1)} %all_to_all.11.recv_ref), custom_call_target="tpu_custom_call" | custom-call | tf_op jit(solution)/shard_map/unpack/pallas_call | solution.py:302
Async XLA Ops:
  0.0 0.7 %copy-start.4 = (f32[1,9,8]{1,2,0:T(8,128)S(1)}, f32[1,9,8]{1,2,0:T(8,128)}, u32[]{:S(2)}) copy-start(f32[1,9,8]{1,2,0:T(8,128)} %param.12) | copy-start | bytes 868
  0.0 0.7 %copy-start.3 = (f32[1,8,9]{2,1,0:T(8,128)S(1)}, f32[1,8,9]{2,1,0:T(8,128)}, u32[]{:S(2)}) copy-start(f32[1,8,9]{2,1,0:T(8,128)} %param.10) | copy-start | bytes 868
  0.7 0.8 %copy-start = (f32[1,8,9,32]{3,1,2,0:T(8,128)S(1)}, f32[1,8,9,32]{3,1,2,0:T(8,128)}, u32[]{:S(2)}) copy-start(f32[1,8,9,32]{3,1,2,0:T(8,128)} %param.9) | copy-start | bytes 27652
  1.5 0.8 %copy-start.1 = (f32[1,9,8,32]{3,2,1,0:T(8,128)S(1)}, f32[1,9,8,32]{3,2,1,0:T(8,128)}, u32[]{:S(2)}) copy-start(f32[1,9,8,32]{3,2,1,0:T(8,128)} %param.11) | copy-start | bytes 27652
  2.2 0.8 %copy-start.2 = (f32[1,8,8,128]{3,2,1,0:T(8,128)S(1)}, f32[1,8,8,128]{3,2,1,0:T(8,128)}, u32[]{:S(2)}) copy-start(f32[1,8,8,128]{3,2,1,0:T(8,128)} %param.8) | copy-start | bytes 98308
  3.0 0.7 %copy-start.5 = (f32[1,8,8]{2,1,0:T(8,128)S(1)}, f32[1,8,8]{2,1,0:T(8,128)}, u32[]{:S(2)}) copy-start(f32[1,8,8]{2,1,0:T(8,128)} %param.13) | copy-start | bytes 772
  4.3 15.5 %copy-start.6 = (s32[2,4]{1,0:T(2,128)S(1)}, s32[2,4]{1,0:T(2,128)}, u32[]{:S(2)}) copy-start(s32[2,4]{1,0:T(2,128)} %partner_ref.1) | copy-start | bytes 100
  4.3 15.5 %copy-start.7 = (s32[2,4]{1,0:T(2,128)S(1)}, s32[2,4]{1,0:T(2,128)}, u32[]{:S(2)}) copy-start(s32[2,4]{1,0:T(2,128)} %flip_ref.1) | copy-start | bytes 100

commit v3 on v2

--- a/solution.py
+++ b/solution.py
@@ -8,11 +8,12 @@
 from jax.sharding import PartitionSpec as P
 
 STEPS = 2
-AXES = ("face", "ty", "tx")
+AXES = ("ty", "face", "tx")
 PARTS = 4
 PAD = 16
 VMEM = pl.BlockSpec(memory_space=pltpu.VMEM)
 SMEM = pl.BlockSpec(memory_space=pltpu.SMEM)
+HBM = pl.BlockSpec(memory_space=pltpu.HBM)
 
 
 def loop(count, body):
@@ -31,13 +32,23 @@
     return jnp.concatenate(split_parts(block.T, rows, 0), axis=1)
 
 
-def pack_kernel(cot_ref, cx_ref, ex_ref, cy_ref, ey_ref, area_ref, send_ref, rows_ref):
+def pack_kernel(*refs):
+    sources, send_ref, rows_ref, sems = refs[:6], refs[6], refs[7], refs[14]
+    cot_ref, cx_ref, ex_ref, cy_ref, ey_ref, area_ref = refs[8:14]
+    copies = [
+        pltpu.make_async_copy(source, target, sems.at[i])
+        for i, (source, target) in enumerate(zip(sources, refs[8:14]))
+    ]
+    for copy in copies:
+        copy.start()
     cy, cx, lanes = cot_ref.shape
     levels = lanes // PARTS
     group = rows_ref.shape[1] // cx
     place = [
         pl.ds(pl.multiple_of((lax.axis_index("tx") + j) % group * cx, cx), cx) for j in range(3)
     ]
+    for copy in copies:
+        copy.wait()
     area = area_ref[...]
     scale_x = [ex_ref[:, i : i + cx] / area for i in range(2)]
     scale_y = [ey_ref[:, i : i + cy] / area.T for i in range(2)]
@@ -65,19 +76,18 @@
         send_ref[:, y, :] = turned(rows_ref[y], levels)
 
 
-def unpack_kernel(recv_ref, out_ref, rows_ref):
-    cy, cx, _ = out_ref.shape
-    group = rows_ref.shape[1] // (PARTS * cx)
-    place = lax.axis_index("tx") % group
-    for y in range(cy):
-        rows_ref[y] = recv_ref[:, y, :].T
-        out_ref[y] = jnp.concatenate(
-            [
-                rows_ref[y, pl.ds(pl.multiple_of((q * group + place) * cx, cx), cx), :]
-                for q in range(PARTS)
-            ],
-            axis=1,
-        )
+def unpack_kernel(recv_ref, out_ref):
+    cy, cx, lanes = out_ref.shape
+    levels = lanes // PARTS
+    group = 128 // (PARTS * cx)
+    half = 8 // group
+    count = cy // group
+    for r in range(count):
+        block = recv_ref[pl.ds(r, levels, stride=count), :].T
+        for b in range(group):
+            out_ref[r // half * 8 + b * half + r % half] = jnp.concatenate(
+                [block[(q * group + b) * cx : (q * group + b + 1) * cx] for q in range(PARTS)], axis=1
+            )
 
 
 def stencil(coefs, side):
@@ -131,7 +141,7 @@
     place_id = lane_id // cx % group
 
     def row_block(i):
-        f, ty = i // tiles_high, i % tiles_high
+        f, ty = i % faces, i // faces
         start = ty * cy
         return f, pl.ds(start if isinstance(i, int) else pl.multiple_of(start, 8), cy)
 
@@ -223,19 +233,42 @@
         sweep(1)
         sweep(0)
 
+    half = 8 // group
+    row_id = lax.broadcasted_iota(jnp.int32, (8, slot_lanes), 0) // half
+    place = lax.broadcasted_iota(jnp.int32, (8, slot_lanes), 1) // cx % group
+
+    def tiles_to_rows(block):
+        bit = 1
+        while bit < group:
+            down = pltpu.roll(pltpu.roll(block, 8 - half * bit, 0), bit * cx, 1)
+            up = pltpu.roll(pltpu.roll(block, half * bit, 0), slot_lanes - bit * cx, 1)
+            a, b = row_id // bit % 2, place // bit % 2
+            block = jnp.where(a == b, block, jnp.where(a == 0, down, up))
+            bit *= 2
+        return block
+
+    count = cy // group
+
     def hand_out(i):
         f, rows = row_block(i)
-        block = field[f, rows, :]
-        for first in range(0, tiles_wide, group):
-            if group == tiles_wide:
-                value = block
-            else:
-                value = jnp.concatenate(
-                    [part[:, first * cx : first * cx + span] for part in split_parts(block, side, 1)],
-                    axis=1,
-                )
-            for tx in range(first, first + group):
-                out_ref[i * tiles_wide + tx] = value
+        strip = field[f, rows, :]
+        for part in range(0, cy, 8):
+            block = strip[part : part + 8]
+            for first in range(0, tiles_wide, group):
+                if group == tiles_wide:
+                    value = block
+                else:
+                    value = jnp.concatenate(
+                        [piece[:, first * cx : first * cx + span] for piece in split_parts(block, side, 1)],
+                        axis=1,
+                    )
+                value = tiles_to_rows(value)
+                base = (i * tiles_wide + first) * count
+                if cy == 8:
+                    out_ref[pl.ds(base if isinstance(i, int) else pl.multiple_of(base, 8), 8), :] = value
+                else:
+                    for a in range(group):
+                        out_ref[pl.ds(base + a * count + part // 8 * half, half), :] = value[a * half : (a + 1) * half]
 
     loop(faces * tiles_high, hand_out)
 
@@ -249,28 +282,19 @@
     cells = cotangent[0]
     cy, cx, lanes = cells.shape
     levels = courant_x.shape[-1]
-    faces, tiles_high, tiles_wide = (lax.axis_size(axis) for axis in AXES)
+    faces, tiles_high, tiles_wide = (lax.axis_size(axis) for axis in ("face", "ty", "tx"))
     devices = faces * tiles_high * tiles_wide
     side = cx * tiles_wide
     width = PARTS * side
     group = 128 // (PARTS * cx)
     if lanes != PARTS * levels or devices % levels or side != cy * tiles_high:
         raise ValueError("unsupported sizes")
-    if cx % 8 or cy % 8 or group < 3 or tiles_wide % group or 128 % side:
+    if cx % 8 or cy % 8 or group != 4 or tiles_wide % group or 128 % side:
         raise ValueError("unsupported tile")
     f32 = jnp.float32
     slot = PARTS * group * cx
 
-    pack_rows = (cy, group * cx, lanes)
-    send = pl.pallas_call(
-        pack_kernel,
-        out_shape=jax.ShapeDtypeStruct((levels, cy, slot), f32),
-        in_specs=[VMEM] * 6,
-        out_specs=VMEM,
-        scratch_shapes=[pltpu.VMEM(pack_rows, f32)],
-        compiler_params=grant(*[cells.shape] * 4, pack_rows, (levels, cy, slot)),
-        name="pack",
-    )(
+    arguments = (
         cells,
         jnp.swapaxes(courant_x[0], 0, 1),
         edge_x[0],
@@ -278,6 +302,20 @@
         jnp.swapaxes(edge_y[0], 0, 1),
         cell_area[0],
     )
+    pack_rows = (cy, group * cx, lanes)
+    send = pl.pallas_call(
+        pack_kernel,
+        out_shape=jax.ShapeDtypeStruct((levels, cy, slot), f32),
+        in_specs=[HBM] * 6,
+        out_specs=VMEM,
+        scratch_shapes=[
+            pltpu.VMEM(pack_rows, f32),
+            *[pltpu.VMEM(argument.shape, f32) for argument in arguments],
+            pltpu.SemaphoreType.DMA((6,)),
+        ],
+        compiler_params=grant(*[cells.shape] * 4, pack_rows, (levels, cy, slot)),
+        name="pack",
+    )(*(pltpu.with_memory_space_constraint(argument, pltpu.HBM) for argument in arguments))
     if devices > levels:
         send = jnp.tile(send, (devices // levels, 1, 1))
     spheres = lax.all_to_all(send, AXES, 0, 0, tiled=True)
@@ -288,26 +326,25 @@
         (min(faces, 2), 7, side + 2 * PAD, width),
         (2, 2, faces, 2, 8, width),
     ]
+    back = (devices * cy // group, slot)
     result = pl.pallas_call(
         functools.partial(sphere_kernel, tiles_high, tiles_wide),
-        out_shape=jax.ShapeDtypeStruct((devices, cy, slot), f32),
+        out_shape=jax.ShapeDtypeStruct(back, f32),
         in_specs=[SMEM, SMEM, VMEM],
         out_specs=VMEM,
         scratch_shapes=[pltpu.VMEM(shape, f32) for shape in scratch],
-        compiler_params=grant(*[(devices, cy, slot)] * 2, *scratch),
+        compiler_params=grant((devices, cy, slot), back, *scratch),
         name="sphere",
     )(seam_partner, seam_flip, spheres)
-    back = lax.all_to_all(result, AXES, 0, 0, tiled=True)[:levels]
-    unpack_rows = (cy, slot, levels)
+    strips = lax.all_to_all(result, AXES, 0, 0, tiled=True)[: levels * cy // group]
     return pl.pallas_call(
         unpack_kernel,
-        out_shape=jax.ShapeDtypeStruct((cy, cx, lanes), f32),
+        out_shape=jax.ShapeDtypeStruct(cells.shape, f32),
         in_specs=[VMEM],
         out_specs=VMEM,
-        scratch_shapes=[pltpu.VMEM(unpack_rows, f32)],
-        compiler_params=grant(cells.shape, back.shape, unpack_rows),
+        compiler_params=grant(cells.shape, strips.shape),
         name="unpack",
-    )(back)[None]
+    )(strips)[None]
 
 
 def solution(mesh):

time: 33.4 us -> 28.9 us (0.87)
  local copies, waits for them, and re-layouts: 3.69 us -> 0.01 us
  blocking collectives: 25.6 us -> 24.2 us
  Pallas kernels: 3.67 us -> 4.45 us
    unnamed x16 -> x4, local copies, waits for them, and re-layouts: 3.69 us -> 0.01 us
    pallas_call x1, Pallas kernels: 0.63 us -> 1.51 us  [on_device(): pl.pallas_call(pack_kernel, out_shape=jax.ShapeDtypeStruct((levels, cy, s...]
    all_to_all x1, blocking collectives: 10.1 us -> 9.23 us  [on_device(): lax.all_to_all(result, AXES, 0, 0, tiled=True)[:levels * cy // group]]
    all_to_all x1, blocking collectives: 15.5 us -> 14.9 us  [on_device(): spheres = lax.all_to_all(send, AXES, 0, 0, tiled=True)]
where the time goes in v3:
time: 28.9 us; the launch traced here: 28.7 us
  blocking collectives  24.2 us (84%)
  Pallas kernels  4.45 us (15%)
    all_to_all x1, blocking collectives, on_device(): spheres = lax.all_to_all(send, AXES, 0, 0, tiled=True)  14.9 us
    all_to_all x1, blocking collectives, on_device(): lax.all_to_all(result, AXES, 0, 0, tiled=True)[:levels * cy // group]  9.23 us
    pallas_call x1, Pallas kernels, on_device(): pl.pallas_call(functools.partial(sphere_kernel, tiles_high, tiles_wide),...  2.14 us
    pallas_call x1, Pallas kernels, on_device(): pl.pallas_call(pack_kernel, out_shape=jax.ShapeDtypeStruct((levels, cy, s...  1.51 us
    pallas_call x1, Pallas kernels, on_device(): pl.pallas_call(unpack_kernel, out_shape=jax.ShapeDtypeStruct(cells.shape,...  0.79 us

profile of v3, /device:TPU:0, one launch (start us, length us, event | category | flops | bytes accessed | tf_op | source)
XLA Modules:
  0.0 28.7 jit_solution(14987435455584043961)
XLA Ops:
  0.0 1.5 %pack.1 = f32[32,8,128]{2,1,0:T(8,128)S(1)} custom-call(f32[8,8,128]{2,1,0:T(8,128)} %bitcast.17, f32[9,8,32]{2,1,0:T(8,128)} %bitcast.15, f32[8,9]{1,0:T(8,128)} %bitcast.18, f32[9,8,32]{2,1,0:T(8,128)} %bitcast.16, f32[8,9]{1,0:T(8,128)} %bitcast.19, f32[8,8]{1,0:T(8,128)} %bitcast.20), custom_call_target="tpu_custom_call" | custom-call | tf_op jit(solution)/shard_map/pack/pallas_call | solution.py:306
  1.5 0.0 copy-start
  1.5 0.0 copy-start.1
  1.5 14.9 %all_to_all.16.recv_ref = f32[32,8,128]{2,1,0:T(8,128)S(1)} all-to-all(f32[32,8,128]{2,1,0:T(8,128)S(1)} %pack.1), channel_id=1, replica_groups=mesh['face'=2,'ty'=4,'tx'=4] {'ty','face','tx'}, dimensions={0} | all-to-all | bytes 262144 | tf_op jit(solution)/shard_map/all_to_all | solution.py:321
  16.5 0.0 copy-done
  16.5 0.0 copy-done.1
  16.5 2.1 %sphere.1 = f32[64,128]{1,0:T(8,128)S(1)} custom-call(s32[2,4]{1,0:T(2,128)S(1)} %copy-done, s32[2,4]{1,0:T(2,128)S(1)} %copy-done.1, f32[32,8,128]{2,1,0:T(8,128)S(1)} %all_to_all.16.recv_ref), custom_call_target="tpu_custom_call" | custom-call | tf_op jit(solution)/shard_map/sphere/pallas_call | solution.py:330
  18.6 9.2 %all_to_all.17 = f32[32,2,128]{2,1,0:T(2,128)S(1)} all-to-all(f32[32,2,128]{2,1,0:T(2,128)S(1)} %bitcast.14), channel_id=1, replica_groups=mesh['face'=2,'ty'=4,'tx'=4] {'ty','face','tx'}, dimensions={0} | all-to-all | bytes 65536 | tf_op jit(solution)/shard_map/all_to_all | solution.py:339
  27.9 0.8 %unpack.1 = f32[8,8,128]{2,1,0:T(8,128)} custom-call(f32[64,128]{1,0:T(8,128)S(1)} %bitcast.13), custom_call_target="tpu_custom_call" | custom-call | tf_op jit(solution)/shard_map/unpack/pallas_call | solution.py:340
Async XLA Ops:
  1.5 15.0 %copy-start = (s32[2,4]{1,0:T(2,128)S(1)}, s32[2,4]{1,0:T(2,128)}, u32[]{:S(2)}) copy-start(s32[2,4]{1,0:T(2,128)} %partner_ref.1) | copy-start | bytes 100
  1.5 15.0 %copy-start.1 = (s32[2,4]{1,0:T(2,128)S(1)}, s32[2,4]{1,0:T(2,128)}, u32[]{:S(2)}) copy-start(s32[2,4]{1,0:T(2,128)} %flip_ref.1) | copy-start | bytes 100

commit v4 on v3

--- a/solution.py
+++ b/solution.py
@@ -1,4 +1,5 @@
 import functools
+import math
 
 import jax
 import jax.numpy as jnp
@@ -12,7 +13,6 @@
 PARTS = 4
 PAD = 16
 VMEM = pl.BlockSpec(memory_space=pltpu.VMEM)
-SMEM = pl.BlockSpec(memory_space=pltpu.SMEM)
 HBM = pl.BlockSpec(memory_space=pltpu.HBM)
 
 
@@ -43,37 +43,30 @@
         copy.start()
     cy, cx, lanes = cot_ref.shape
     levels = lanes // PARTS
-    group = rows_ref.shape[1] // cx
-    place = [
-        pl.ds(pl.multiple_of((lax.axis_index("tx") + j) % group * cx, cx), cx) for j in range(3)
-    ]
+    group = 128 // (PARTS * cx)
+    span = group * cx
+    place = [pl.multiple_of(((lax.axis_index("tx") + j) & (group - 1)) * cx, cx) for j in range(3)]
     for copy in copies:
         copy.wait()
     area = area_ref[...]
     scale_x = [ex_ref[:, i : i + cx] / area for i in range(2)]
     scale_y = [ey_ref[:, i : i + cy] / area.T for i in range(2)]
-    if group > 3:
-        rows_ref[...] = jnp.zeros_like(rows_ref)
-
-    by_x = []
+
     for x in range(cx):
         pieces = []
         for i in range(2):
             c = cx_ref[x + i]
             pieces += [c, c * scale_x[i][:, x : x + 1]]
-        by_x.append(jnp.concatenate(pieces, axis=1))
-    by_x = jnp.stack(by_x)
-    for y0 in range(0, cy, 8):
-        rows_ref[y0 : y0 + 8, place[1], :] = jnp.swapaxes(by_x[:, y0 : y0 + 8], 0, 1)
+        rows_ref[pl.ds(place[1] + x, cy, stride=span), :] = jnp.concatenate(pieces, axis=1)
     for y in range(cy):
         pieces = []
         for i in range(2):
             c = cy_ref[y + i]
             pieces += [c, c * scale_y[i][:, y : y + 1]]
-        rows_ref[y, place[2], :] = jnp.concatenate(pieces, axis=1)
-        rows_ref[y, place[0], :] = cot_ref[y]
+        rows_ref[pl.ds(y * span + place[2], cx), :] = jnp.concatenate(pieces, axis=1)
+        rows_ref[pl.ds(y * span + place[0], cx), :] = cot_ref[y]
     for y in range(cy):
-        send_ref[:, y, :] = turned(rows_ref[y], levels)
+        send_ref[pl.ds(y, levels, stride=cy), :] = turned(rows_ref[y * span : (y + 1) * span], levels)
 
 
 def unpack_kernel(recv_ref, out_ref):
@@ -129,8 +122,27 @@
 
 
 def sphere_kernel(
-    tiles_high, tiles_wide, partner_ref, flip_ref, recv_ref, out_ref, beta, acc, field, prod, rim
+    tiles_high,
+    tiles_wide,
+    partner_hbm,
+    flip_hbm,
+    recv_ref,
+    out_ref,
+    beta,
+    acc,
+    field,
+    prod,
+    rim,
+    partner_ref,
+    flip_ref,
+    sems,
 ):
+    copies = [
+        pltpu.make_async_copy(partner_hbm, partner_ref, sems.at[0]),
+        pltpu.make_async_copy(flip_hbm, flip_ref, sems.at[1]),
+    ]
+    for copy in copies:
+        copy.start()
     faces, side, lanes = field.shape
     cy, cx = side // tiles_high, side // tiles_wide
     slots = prod.shape[0]
@@ -138,7 +150,7 @@
     group = slot_lanes // (PARTS * cx)
     span = group * cx
     lane_id = lax.broadcasted_iota(jnp.int32, (cy, slot_lanes), 1)
-    place_id = lane_id // cx % group
+    place_id = (lane_id >> (cx.bit_length() - 1)) & (group - 1)
 
     def row_block(i):
         f, ty = i % faces, i // faces
@@ -180,69 +192,91 @@
     prod[...] = jnp.zeros_like(prod)
     rim[...] = jnp.zeros_like(rim)
     mirror_id = lax.broadcasted_iota(jnp.int32, (8, 128), 1)
-    mirror_id = mirror_id // side * side + (side - 1 - mirror_id % side)
+    mirror_id = mirror_id ^ (side - 1)
+    upside_id = 7 - lax.broadcasted_iota(jnp.int32, (8, 128), 0)
+
+    def by_lanes(fun, value):
+        return jnp.concatenate([fun(value[:, at : at + 128]) for at in range(0, lanes, 128)], axis=1)
+
+    def mirrored(value):
+        return by_lanes(lambda chunk: jnp.take_along_axis(chunk, mirror_id, axis=1), value)
+
+    def upside(value):
+        return by_lanes(lambda chunk: jnp.take_along_axis(chunk, upside_id, axis=0), value)
+
+    for copy in copies:
+        copy.wait()
 
     def sweep(d):
         def apply(f):
             cells = field[f]
             here = prod.at[f % slots]
-            total = None
+            middle = beta[d, 3, f] * cells
             for k in range(7):
-                here[k, PAD : PAD + side, :] = beta[d, k, f] * cells
-            for k in range(7):
-                start = PAD - 8 - (k - 3)
-                term = here[k, start : start + side + 16, :]
-                total = term if total is None else total + term
-            acc[d, f] = total[8 : 8 + side]
-            acc[1 - d, f] = jnp.zeros((side, lanes), jnp.float32)
-            for low in range(2):
-                rows = total[0:8] if low else total[side + 8 :]
-                rim[0, low, f, low] = rows
-                for depth in range(3):
-                    source, target = (7 - depth, depth) if low else (depth, 7 - depth)
-                    rim[0, 1 - low, f, low, target : target + 1, :] = rows[source : source + 1]
+                if k != 3:
+                    here[k, PAD : PAD + side, :] = beta[d, k, f] * cells
+            before, after = None, None
+            for k in (0, 1, 2, 4, 5, 6):
+                shift = k - 3
+                middle = middle + here[k, PAD - shift : PAD - shift + side, :]
+                if shift < 0:
+                    term = here[k, PAD - 8 - shift : PAD - shift, :]
+                    before = term if before is None else before + term
+                else:
+                    term = here[k, PAD + side - shift : PAD + side + 8 - shift, :]
+                    after = term if after is None else after + term
+            acc[0, f] = middle
+            for low, rows in ((0, after), (1, before)):
+                orders = (rows, upside(rows))
                 for order in range(2):
-                    value = rim[0, order, f, low]
-                    rim[1, order, f, low] = jnp.concatenate(
-                        [
-                            jnp.take_along_axis(value[:, at : at + 128], mirror_id, axis=1)
-                            for at in range(0, lanes, 128)
-                        ],
-                        axis=1,
-                    )
+                    value = orders[order ^ low]
+                    rim[0, order, f, low] = value
+                    rim[1, order, f, low] = mirrored(value)
 
         loop(faces, apply)
-        for f in range(faces):
-            for low in range(2):
-                edge = d + 2 * low
-                code = partner_ref[f, edge]
-                other, border = code // 4, code % 4
-                high = jnp.where(border < 2, 1, 0)
-                rows = pl.ds(pl.multiple_of(high * (side - 8), 8), 8)
-                layout = border % 2
-                acc[layout, other, rows, :] = (
-                    acc[layout, other, rows, :] + rim[flip_ref[f, edge], high, f, low]
-                )
-
-        def merge(f):
-            field[f] = turned(acc[d, f], side) + acc[1 - d, f]
-
-        loop(faces, merge)
+
+        def seam(f, edge):
+            code = partner_ref[f, edge]
+            value = rim[flip_ref[f, edge], int(edge < 2), code >> 2, (code & 3) >> 1]
+            return jnp.where((code & 1) == d, value, 0.0)
+
+        def with_seams(value, f, axis):
+            return jnp.concatenate(
+                [
+                    value[0:8] + seam(f, axis + 2),
+                    value[8 : side - 8],
+                    value[side - 8 :] + seam(f, axis),
+                ],
+                axis=0,
+            )
+
+        if faces * side <= 128:
+            block = jnp.concatenate([with_seams(acc[0, f], f, d) for f in range(faces)], axis=0).T
+            for f in range(faces):
+                columns = block[:, f * side : (f + 1) * side]
+                value = jnp.concatenate(split_parts(columns, side, 0), axis=1)
+                field[f] = with_seams(value, f, 1 - d)
+        else:
+
+            def merge(f):
+                field[f] = with_seams(turned(with_seams(acc[0, f], f, d), side), f, 1 - d)
+
+            loop(faces, merge)
 
     for step in range(STEPS):
         sweep(1)
         sweep(0)
 
     half = 8 // group
-    row_id = lax.broadcasted_iota(jnp.int32, (8, slot_lanes), 0) // half
-    place = lax.broadcasted_iota(jnp.int32, (8, slot_lanes), 1) // cx % group
+    row_id = lax.broadcasted_iota(jnp.int32, (8, slot_lanes), 0) >> (half.bit_length() - 1)
+    place = place_id[0:8]
 
     def tiles_to_rows(block):
         bit = 1
         while bit < group:
             down = pltpu.roll(pltpu.roll(block, 8 - half * bit, 0), bit * cx, 1)
             up = pltpu.roll(pltpu.roll(block, half * bit, 0), slot_lanes - bit * cx, 1)
-            a, b = row_id // bit % 2, place // bit % 2
+            a, b = row_id & bit, place & bit
             block = jnp.where(a == b, block, jnp.where(a == 0, down, up))
             bit *= 2
         return block
@@ -273,9 +307,15 @@
     loop(faces * tiles_high, hand_out)
 
 
-def grant(*blocks):
-    words = sum(functools.reduce(lambda a, b: a * b, (*shape[:-2], -(-shape[-2] // 8) * 8, -(-shape[-1] // 128) * 128)) for shape in blocks)
-    return pltpu.CompilerParams(vmem_limit_bytes=5 * words + (2 << 20))
+def in_hbm(array):
+    return pltpu.with_memory_space_constraint(array, pltpu.HBM)
+
+
+def grant(*shapes):
+    size = 0
+    for *major, rows, columns in shapes:
+        size += 4 * math.prod(major) * (-(-rows // 8) * 8) * (-(-columns // 128) * 128)
+    return pltpu.CompilerParams(vmem_limit_bytes=size + size // 4 + (2 << 20))
 
 
 def on_device(cotangent, courant_x, edge_x, courant_y, edge_y, cell_area, seam_partner, seam_flip):
@@ -289,7 +329,7 @@
     group = 128 // (PARTS * cx)
     if lanes != PARTS * levels or devices % levels or side != cy * tiles_high:
         raise ValueError("unsupported sizes")
-    if cx % 8 or cy % 8 or group != 4 or tiles_wide % group or 128 % side:
+    if cx != 8 or cy % 8 or tiles_wide % group or 128 % side:
         raise ValueError("unsupported tile")
     f32 = jnp.float32
     slot = PARTS * group * cx
@@ -302,10 +342,10 @@
         jnp.swapaxes(edge_y[0], 0, 1),
         cell_area[0],
     )
-    pack_rows = (cy, group * cx, lanes)
+    pack_rows = (cy * group * cx, lanes)
     send = pl.pallas_call(
         pack_kernel,
-        out_shape=jax.ShapeDtypeStruct((levels, cy, slot), f32),
+        out_shape=jax.ShapeDtypeStruct((levels * cy, slot), f32),
         in_specs=[HBM] * 6,
         out_specs=VMEM,
         scratch_shapes=[
@@ -315,10 +355,10 @@
         ],
         compiler_params=grant(*[cells.shape] * 4, pack_rows, (levels, cy, slot)),
         name="pack",
-    )(*(pltpu.with_memory_space_constraint(argument, pltpu.HBM) for argument in arguments))
+    )(*map(in_hbm, arguments))
     if devices > levels:
-        send = jnp.tile(send, (devices // levels, 1, 1))
-    spheres = lax.all_to_all(send, AXES, 0, 0, tiled=True)
+        send = jnp.tile(send, (devices // levels, 1))
+    spheres = lax.all_to_all(send.reshape(devices, cy, slot), AXES, 0, 0, tiled=True)
     scratch = [
         (2, 7, faces, side, width),
         (2, faces, side, width),
@@ -330,12 +370,17 @@
     result = pl.pallas_call(
         functools.partial(sphere_kernel, tiles_high, tiles_wide),
         out_shape=jax.ShapeDtypeStruct(back, f32),
-        in_specs=[SMEM, SMEM, VMEM],
+        in_specs=[HBM, HBM, VMEM],
         out_specs=VMEM,
-        scratch_shapes=[pltpu.VMEM(shape, f32) for shape in scratch],
+        scratch_shapes=[
+            *[pltpu.VMEM(shape, f32) for shape in scratch],
+            pltpu.SMEM(seam_partner.shape, jnp.int32),
+            pltpu.SMEM(seam_flip.shape, jnp.int32),
+            pltpu.SemaphoreType.DMA((2,)),
+        ],
         compiler_params=grant((devices, cy, slot), back, *scratch),
         name="sphere",
-    )(seam_partner, seam_flip, spheres)
+    )(in_hbm(seam_partner), in_hbm(seam_flip), spheres)
     strips = lax.all_to_all(result, AXES, 0, 0, tiled=True)[: levels * cy // group]
     return pl.pallas_call(
         unpack_kernel,

time: 28.9 us -> 28.7 us (level)
  no operation moved by 1% of the time
where the time goes in v4:
time: 28.7 us; the launch traced here: 28.4 us
  blocking collectives  24.2 us (84%)
  Pallas kernels  4.24 us (15%)
    all_to_all x1, blocking collectives, on_device(): lax.all_to_all(send.reshape(devices, cy, slot), AXES, 0, 0, tiled=True)  14.9 us
    all_to_all x1, blocking collectives, on_device(): lax.all_to_all(result, AXES, 0, 0, tiled=True)[:levels * cy // group]  9.23 us
    pallas_call x1, Pallas kernels, on_device(): pl.pallas_call(functools.partial(sphere_kernel, tiles_high, tiles_wide),...  1.95 us
    pallas_call x1, Pallas kernels, on_device(): pl.pallas_call(pack_kernel, out_shape=jax.ShapeDtypeStruct((levels * cy,...  1.5 us
    pallas_call x1, Pallas kernels, on_device(): pl.pallas_call(unpack_kernel, out_shape=jax.ShapeDtypeStruct(cells.shape,...  0.79 us

profile of v4, /device:TPU:0, one launch (start us, length us, event | category | flops | bytes accessed | tf_op | source)
XLA Modules:
  0.0 28.4 jit_solution(11778367422534254346)
XLA Ops:
  0.0 1.5 %pack.1 = f32[256,128]{1,0:T(8,128)S(1)} custom-call(f32[8,8,128]{2,1,0:T(8,128)} %bitcast.19, f32[9,8,32]{2,1,0:T(8,128)} %bitcast.17, f32[8,9]{1,0:T(8,128)} %bitcast.20, f32[9,8,32]{2,1,0:T(8,128)} %bitcast.18, f32[8,9]{1,0:T(8,128)} %bitcast.21, f32[8,8]{1,0:T(8,128)} %bitcast.22), custom_call_target="tpu_custom_call" | custom-call | tf_op jit(solution)/shard_map/pack/pallas_call | solution.py:346
  1.5 14.9 %all_to_all.16.recv_ref = f32[32,8,128]{2,1,0:T(8,128)S(1)} all-to-all(f32[32,8,128]{2,1,0:T(8,128)S(1)} %bitcast.14), channel_id=1, replica_groups=mesh['face'=2,'ty'=4,'tx'=4] {'ty','face','tx'}, dimensions={0} | all-to-all | bytes 262144 | tf_op jit(solution)/shard_map/all_to_all | solution.py:361
  16.4 2.0 %sphere.1 = f32[64,128]{1,0:T(8,128)S(1)} custom-call(s32[2,4]{1,0:T(2,128)} %partner_hbm.1, s32[2,4]{1,0:T(2,128)} %flip_hbm.1, f32[32,8,128]{2,1,0:T(8,128)S(1)} %all_to_all.16.recv_ref), custom_call_target="tpu_custom_call" | custom-call | tf_op jit(solution)/shard_map/sphere/pallas_call | solution.py:370
  18.4 9.2 %all_to_all.17 = f32[32,2,128]{2,1,0:T(2,128)S(1)} all-to-all(f32[32,2,128]{2,1,0:T(2,128)S(1)} %bitcast.16), channel_id=1, replica_groups=mesh['face'=2,'ty'=4,'tx'=4] {'ty','face','tx'}, dimensions={0} | all-to-all | bytes 65536 | tf_op jit(solution)/shard_map/all_to_all | solution.py:384
  27.6 0.8 %unpack.1 = f32[8,8,128]{2,1,0:T(8,128)} custom-call(f32[64,128]{1,0:T(8,128)S(1)} %bitcast.15), custom_call_target="tpu_custom_call" | custom-call | tf_op jit(solution)/shard_map/unpack/pallas_call | solution.py:385

commit v5 on v4

--- a/solution.py
+++ b/solution.py
@@ -32,41 +32,55 @@
     return jnp.concatenate(split_parts(block.T, rows, 0), axis=1)
 
 
-def pack_kernel(*refs):
-    sources, send_ref, rows_ref, sems = refs[:6], refs[6], refs[7], refs[14]
-    cot_ref, cx_ref, ex_ref, cy_ref, ey_ref, area_ref = refs[8:14]
-    copies = [
-        pltpu.make_async_copy(source, target, sems.at[i])
-        for i, (source, target) in enumerate(zip(sources, refs[8:14]))
-    ]
-    for copy in copies:
-        copy.start()
-    cy, cx, lanes = cot_ref.shape
+def pack_kernel(
+    cot_hbm, cx_hbm, ex_hbm, cy_hbm, ey_hbm, area_hbm, send_ref, rows_ref, cx_ref, ex_ref, cy_ref, ey_ref, area_ref, sems
+):
+    cy, cx = area_ref.shape
+    lanes = rows_ref.shape[1]
     levels = lanes // PARTS
     group = 128 // (PARTS * cx)
     span = group * cx
     place = [pl.multiple_of(((lax.axis_index("tx") + j) & (group - 1)) * cx, cx) for j in range(3)]
+    copies = [
+        pltpu.make_async_copy(source, target, sems.at[i])
+        for i, (source, target) in enumerate(
+            [(ex_hbm, ex_ref), (ey_hbm, ey_ref), (area_hbm, area_ref), (cx_hbm, cx_ref), (cy_hbm, cy_ref)]
+            + [(cot_hbm.at[y], rows_ref.at[pl.ds(y * span + place[0], cx)]) for y in range(cy)]
+        )
+    ]
+    for copy in copies:
+        copy.start()
     for copy in copies:
         copy.wait()
+
+    for x in range(cx):
+        rows_ref[pl.ds(place[1] + x, cy, stride=span), 0 : 2 * levels] = jnp.concatenate(
+            [cx_ref[x], cx_ref[x + 1]], axis=1
+        )
+    for y in range(cy):
+        rows_ref[pl.ds(y * span + place[1], cx), 2 * levels :] = jnp.concatenate(
+            [cy_ref[y], cy_ref[y + 1]], axis=1
+        )
+
     area = area_ref[...]
-    scale_x = [ex_ref[:, i : i + cx] / area for i in range(2)]
-    scale_y = [ey_ref[:, i : i + cy] / area.T for i in range(2)]
-
-    for x in range(cx):
-        pieces = []
-        for i in range(2):
-            c = cx_ref[x + i]
-            pieces += [c, c * scale_x[i][:, x : x + 1]]
-        rows_ref[pl.ds(place[1] + x, cy, stride=span), :] = jnp.concatenate(pieces, axis=1)
-    for y in range(cy):
-        pieces = []
-        for i in range(2):
-            c = cy_ref[y + i]
-            pieces += [c, c * scale_y[i][:, y : y + 1]]
-        rows_ref[pl.ds(y * span + place[2], cx), :] = jnp.concatenate(pieces, axis=1)
-        rows_ref[pl.ds(y * span + place[0], cx), :] = cot_ref[y]
-    for y in range(cy):
-        send_ref[pl.ds(y, levels, stride=cy), :] = turned(rows_ref[y * span : (y + 1) * span], levels)
+    ey = ey_ref[...].T
+    gap = jnp.zeros((cy, span - cx), jnp.float32)
+    metric = []
+    for length in (ex_ref[:, 0:cx], ex_ref[:, 1 : cx + 1], ey[0:cy], ey[1 : cy + 1]):
+        metric += [length / area, gap]
+    metric = pltpu.roll(jnp.concatenate(metric, axis=1), place[2], 1)
+    lane_id = lax.broadcasted_iota(jnp.int32, (levels, lanes), 1)
+    here = (lane_id & (span - 1)) >> (cx.bit_length() - 1) == place[2] >> (cx.bit_length() - 1)
+
+    for first in range(0, cy, group):
+        block = rows_ref[first * span : (first + group) * span].T
+        for i in range(group):
+            y = first + i
+            row = jnp.concatenate(
+                [block[q * levels : (q + 1) * levels, i * span : (i + 1) * span] for q in range(PARTS)],
+                axis=1,
+            )
+            send_ref[pl.ds(y, levels, stride=cy), :] = jnp.where(here, metric[y : y + 1], row)
 
 
 def unpack_kernel(recv_ref, out_ref):
@@ -83,10 +97,8 @@
             )
 
 
-def stencil(coefs, side):
-    c_low, f_low, c_high, f_high = (
-        jnp.concatenate([part] * PARTS, axis=1) for part in split_parts(coefs, side, 1)
-    )
+def stencil(*parts):
+    c_low, f_low, c_high, f_high = (jnp.concatenate([part] * PARTS, axis=1) for part in parts)
 
     def interface(c, f):
         size = jnp.abs(c)
@@ -129,6 +141,7 @@
     recv_ref,
     out_ref,
     beta,
+    coef,
     acc,
     field,
     prod,
@@ -159,7 +172,8 @@
 
     def assemble(i):
         f, rows = row_block(i)
-        for j, target in enumerate((field, acc.at[0], acc.at[1])):
+        values = []
+        for j in range(3):
             blocks = []
             for first in range(0, tiles_wide, group):
                 tiles = [recv_ref[i * tiles_wide + first + tx] for tx in range(group)]
@@ -172,23 +186,48 @@
                     block = jnp.where(place_id < group - j, ahead, around)
                 blocks.append(block)
             if len(blocks) == 1:
-                value = blocks[0]
+                values.append(blocks[0])
             else:
-                value = jnp.concatenate(
-                    [block[:, q * span : (q + 1) * span] for q in range(PARTS) for block in blocks],
-                    axis=1,
+                values.append(
+                    jnp.concatenate(
+                        [block[:, q * span : (q + 1) * span] for q in range(PARTS) for block in blocks],
+                        axis=1,
+                    )
                 )
-            target[f, rows, :] = value
+        cells, courant, metric = values
+        field[f, rows, :] = cells
+        coef[0, f, rows, :] = courant
+        coef[1, f, rows, :] = courant * metric
 
     loop(faces * tiles_high, assemble)
 
-    def coefficients(f):
-        for k, value in enumerate(stencil(turned(acc[0, f], side), side)):
-            beta[0, k, f] = value
-        for k, value in enumerate(stencil(acc[1, f], side)):
+    def over_groups(body):
+        if faces * side <= 128:
+            body(list(range(faces)))
+        else:
+            loop(faces, lambda f: body([f]))
+
+    def turned_parts(blocks):
+        if len(blocks) == 1:
+            return [split_parts(blocks[0].T, side, 0)]
+        block = jnp.concatenate(blocks, axis=0).T
+        return [
+            split_parts(block[:, i * side : (i + 1) * side], side, 0) for i in range(len(blocks))
+        ]
+
+    def coefficients_x(group_faces):
+        courant = turned_parts([coef[0, f] for f in group_faces])
+        scaled = turned_parts([coef[1, f] for f in group_faces])
+        for f, c, s in zip(group_faces, courant, scaled):
+            for k, value in enumerate(stencil(c[0], s[0], c[1], s[1])):
+                beta[0, k, f] = value
+
+    def coefficients_y(f):
+        c, s = split_parts(coef[0, f], side, 1), split_parts(coef[1, f], side, 1)
+        for k, value in enumerate(stencil(c[2], s[2], c[3], s[3])):
             beta[1, k, f] = value
 
-    loop(faces, coefficients)
+    loop(faces, coefficients_y)
     prod[...] = jnp.zeros_like(prod)
     rim[...] = jnp.zeros_like(rim)
     mirror_id = lax.broadcasted_iota(jnp.int32, (8, 128), 1)
@@ -207,7 +246,7 @@
     for copy in copies:
         copy.wait()
 
-    def sweep(d):
+    def sweep(d, between=None):
         def apply(f):
             cells = field[f]
             here = prod.at[f % slots]
@@ -225,7 +264,7 @@
                 else:
                     term = here[k, PAD + side - shift : PAD + side + 8 - shift, :]
                     after = term if after is None else after + term
-            acc[0, f] = middle
+            acc[f] = middle
             for low, rows in ((0, after), (1, before)):
                 orders = (rows, upside(rows))
                 for order in range(2):
@@ -234,6 +273,8 @@
                     rim[1, order, f, low] = mirrored(value)
 
         loop(faces, apply)
+        if between:
+            between()
 
         def seam(f, edge):
             code = partner_ref[f, edge]
@@ -250,21 +291,15 @@
                 axis=0,
             )
 
-        if faces * side <= 128:
-            block = jnp.concatenate([with_seams(acc[0, f], f, d) for f in range(faces)], axis=0).T
-            for f in range(faces):
-                columns = block[:, f * side : (f + 1) * side]
-                value = jnp.concatenate(split_parts(columns, side, 0), axis=1)
-                field[f] = with_seams(value, f, 1 - d)
-        else:
-
-            def merge(f):
-                field[f] = with_seams(turned(with_seams(acc[0, f], f, d), side), f, 1 - d)
-
-            loop(faces, merge)
+        def merge(group_faces):
+            blocks = turned_parts([with_seams(acc[f], f, d) for f in group_faces])
+            for f, parts in zip(group_faces, blocks):
+                field[f] = with_seams(jnp.concatenate(parts, axis=1), f, 1 - d)
+
+        over_groups(merge)
 
     for step in range(STEPS):
-        sweep(1)
+        sweep(1, None if step else lambda: over_groups(coefficients_x))
         sweep(0)
 
     half = 8 // group
@@ -350,8 +385,8 @@
         out_specs=VMEM,
         scratch_shapes=[
             pltpu.VMEM(pack_rows, f32),
-            *[pltpu.VMEM(argument.shape, f32) for argument in arguments],
-            pltpu.SemaphoreType.DMA((6,)),
+            *[pltpu.VMEM(argument.shape, f32) for argument in arguments[1:]],
+            pltpu.SemaphoreType.DMA((5 + cy,)),
         ],
         compiler_params=grant(*[cells.shape] * 4, pack_rows, (levels, cy, slot)),
         name="pack",
@@ -362,6 +397,7 @@
     scratch = [
         (2, 7, faces, side, width),
         (2, faces, side, width),
+        (faces, side, width),
         (faces, side, width),
         (min(faces, 2), 7, side + 2 * PAD, width),
         (2, 2, faces, 2, 8, width),

time: 28.7 us -> 28.7 us (level)
  no operation moved by 1% of the time
where the time goes in v5:
time: 28.7 us; the launch traced here: 28.5 us
  blocking collectives  24.2 us (84%)
  Pallas kernels  4.31 us (15%)
    all_to_all x1, blocking collectives, on_device(): lax.all_to_all(send.reshape(devices, cy, slot), AXES, 0, 0, tiled=True)  14.9 us
    all_to_all x1, blocking collectives, on_device(): lax.all_to_all(result, AXES, 0, 0, tiled=True)[:levels * cy // group]  9.23 us
    pallas_call x1, Pallas kernels, on_device(): pl.pallas_call(functools.partial(sphere_kernel, tiles_high, tiles_wide),...  2.03 us
    pallas_call x1, Pallas kernels, on_device(): pl.pallas_call(pack_kernel, out_shape=jax.ShapeDtypeStruct((levels * cy,...  1.49 us
    pallas_call x1, Pallas kernels, on_device(): pl.pallas_call(unpack_kernel, out_shape=jax.ShapeDtypeStruct(cells.shape,...  0.79 us

profile of v5, /device:TPU:0, one launch (start us, length us, event | category | flops | bytes accessed | tf_op | source)
XLA Modules:
  0.0 28.5 jit_solution(6928015399072256932)
XLA Ops:
  0.0 1.5 %pack.1 = f32[256,128]{1,0:T(8,128)S(1)} custom-call(f32[8,8,128]{2,1,0:T(8,128)} %bitcast.19, f32[9,8,32]{2,1,0:T(8,128)} %bitcast.17, f32[8,9]{1,0:T(8,128)} %bitcast.20, f32[9,8,32]{2,1,0:T(8,128)} %bitcast.18, f32[8,9]{1,0:T(8,128)} %bitcast.21, f32[8,8]{1,0:T(8,128)} %bitcast.22), custom_call_target="tpu_custom_call" | custom-call | tf_op jit(solution)/shard_map/pack/pallas_call | solution.py:381
  1.5 14.9 %all_to_all.16.recv_ref = f32[32,8,128]{2,1,0:T(8,128)S(1)} all-to-all(f32[32,8,128]{2,1,0:T(8,128)S(1)} %bitcast.14), channel_id=1, replica_groups=mesh['face'=2,'ty'=4,'tx'=4] {'ty','face','tx'}, dimensions={0} | all-to-all | bytes 262144 | tf_op jit(solution)/shard_map/all_to_all | solution.py:396
  16.4 2.0 %sphere.1 = f32[64,128]{1,0:T(8,128)S(1)} custom-call(s32[2,4]{1,0:T(2,128)} %partner_hbm.1, s32[2,4]{1,0:T(2,128)} %flip_hbm.1, f32[32,8,128]{2,1,0:T(8,128)S(1)} %all_to_all.16.recv_ref), custom_call_target="tpu_custom_call" | custom-call | tf_op jit(solution)/shard_map/sphere/pallas_call | solution.py:406
  18.5 9.2 %all_to_all.17 = f32[32,2,128]{2,1,0:T(2,128)S(1)} all-to-all(f32[32,2,128]{2,1,0:T(2,128)S(1)} %bitcast.16), channel_id=1, replica_groups=mesh['face'=2,'ty'=4,'tx'=4] {'ty','face','tx'}, dimensions={0} | all-to-all | bytes 65536 | tf_op jit(solution)/shard_map/all_to_all | solution.py:420
  27.7 0.8 %unpack.1 = f32[8,8,128]{2,1,0:T(8,128)} custom-call(f32[64,128]{1,0:T(8,128)S(1)} %bitcast.15), custom_call_target="tpu_custom_call" | custom-call | tf_op jit(solution)/shard_map/unpack/pallas_call | solution.py:421

commit v6 on v5

--- a/solution.py
+++ b/solution.py
@@ -243,9 +243,6 @@
     def upside(value):
         return by_lanes(lambda chunk: jnp.take_along_axis(chunk, upside_id, axis=0), value)
 
-    for copy in copies:
-        copy.wait()
-
     def sweep(d, between=None):
         def apply(f):
             cells = field[f]
@@ -298,8 +295,13 @@
 
         over_groups(merge)
 
+    def between():
+        over_groups(coefficients_x)
+        for copy in copies:
+            copy.wait()
+
     for step in range(STEPS):
-        sweep(1, None if step else lambda: over_groups(coefficients_x))
+        sweep(1, None if step else between)
         sweep(0)
 
     half = 8 // group

time: 28.7 us -> 28.6 us (level)
  no operation moved by 1% of the time
where the time goes in v6:
time: 28.6 us; the launch traced here: 28.3 us
  blocking collectives  24.2 us (85%)
  Pallas kernels  4.15 us (15%)
    all_to_all x1, blocking collectives, on_device(): lax.all_to_all(send.reshape(devices, cy, slot), AXES, 0, 0, tiled=True)  14.9 us
    all_to_all x1, blocking collectives, on_device(): lax.all_to_all(result, AXES, 0, 0, tiled=True)[:levels * cy // group]  9.23 us
    pallas_call x1, Pallas kernels, on_device(): pl.pallas_call(functools.partial(sphere_kernel, tiles_high, tiles_wide),...  1.87 us
    pallas_call x1, Pallas kernels, on_device(): pl.pallas_call(pack_kernel, out_shape=jax.ShapeDtypeStruct((levels * cy,...  1.49 us
    pallas_call x1, Pallas kernels, on_device(): pl.pallas_call(unpack_kernel, out_shape=jax.ShapeDtypeStruct(cells.shape,...  0.79 us

profile of v6, /device:TPU:0, one launch (start us, length us, event | category | flops | bytes accessed | tf_op | source)
XLA Modules:
  0.0 28.3 jit_solution(7018904342671819083)
XLA Ops:
  0.0 1.5 %pack.1 = f32[256,128]{1,0:T(8,128)S(1)} custom-call(f32[8,8,128]{2,1,0:T(8,128)} %bitcast.19, f32[9,8,32]{2,1,0:T(8,128)} %bitcast.17, f32[8,9]{1,0:T(8,128)} %bitcast.20, f32[9,8,32]{2,1,0:T(8,128)} %bitcast.18, f32[8,9]{1,0:T(8,128)} %bitcast.21, f32[8,8]{1,0:T(8,128)} %bitcast.22), custom_call_target="tpu_custom_call" | custom-call | tf_op jit(solution)/shard_map/pack/pallas_call | solution.py:383
  1.5 14.9 %all_to_all.16.recv_ref = f32[32,8,128]{2,1,0:T(8,128)S(1)} all-to-all(f32[32,8,128]{2,1,0:T(8,128)S(1)} %bitcast.14), channel_id=1, replica_groups=mesh['face'=2,'ty'=4,'tx'=4] {'ty','face','tx'}, dimensions={0} | all-to-all | bytes 262144 | tf_op jit(solution)/shard_map/all_to_all | solution.py:398
  16.4 1.9 %sphere.1 = f32[64,128]{1,0:T(8,128)S(1)} custom-call(s32[2,4]{1,0:T(2,128)} %partner_hbm.1, s32[2,4]{1,0:T(2,128)} %flip_hbm.1, f32[32,8,128]{2,1,0:T(8,128)S(1)} %all_to_all.16.recv_ref), custom_call_target="tpu_custom_call" | custom-call | tf_op jit(solution)/shard_map/sphere/pallas_call | solution.py:408
  18.3 9.2 %all_to_all.17 = f32[32,2,128]{2,1,0:T(2,128)S(1)} all-to-all(f32[32,2,128]{2,1,0:T(2,128)S(1)} %bitcast.16), channel_id=1, replica_groups=mesh['face'=2,'ty'=4,'tx'=4] {'ty','face','tx'}, dimensions={0} | all-to-all | bytes 65536 | tf_op jit(solution)/shard_map/all_to_all | solution.py:422
  27.5 0.8 %unpack.1 = f32[8,8,128]{2,1,0:T(8,128)} custom-call(f32[64,128]{1,0:T(8,128)S(1)} %bitcast.15), custom_call_target="tpu_custom_call" | custom-call | tf_op jit(solution)/shard_map/unpack/pallas_call | solution.py:423

commit v7 on v6

--- a/solution.py
+++ b/solution.py
@@ -40,12 +40,20 @@
     levels = lanes // PARTS
     group = 128 // (PARTS * cx)
     span = group * cx
-    place = [pl.multiple_of(((lax.axis_index("tx") + j) & (group - 1)) * cx, cx) for j in range(3)]
+    count = cy * 3 // 4
+    place = [pl.multiple_of(((lax.axis_index("tx") + j) & (group - 1)) * cx, cx) for j in range(4)]
+
+    def home(y, j):
+        part, row = y // 8 * 6, y % 8
+        if row < 6:
+            return (part + row) * span + place[j]
+        return (part + (row - 6) * 3 + j) * span + place[3]
+
     copies = [
         pltpu.make_async_copy(source, target, sems.at[i])
         for i, (source, target) in enumerate(
             [(ex_hbm, ex_ref), (ey_hbm, ey_ref), (area_hbm, area_ref), (cx_hbm, cx_ref), (cy_hbm, cy_ref)]
-            + [(cot_hbm.at[y], rows_ref.at[pl.ds(y * span + place[0], cx)]) for y in range(cy)]
+            + [(cot_hbm.at[y], rows_ref.at[pl.ds(home(y, 0), cx)]) for y in range(cy)]
         )
     ]
     for copy in copies:
@@ -54,13 +62,12 @@
         copy.wait()
 
     for x in range(cx):
-        rows_ref[pl.ds(place[1] + x, cy, stride=span), 0 : 2 * levels] = jnp.concatenate(
-            [cx_ref[x], cx_ref[x + 1]], axis=1
-        )
+        value = jnp.concatenate([cx_ref[x], cx_ref[x + 1]], axis=1)
+        for y in range(0, cy, 8):
+            rows_ref[pl.ds(home(y, 1) + x, 6, stride=span), 0 : 2 * levels] = value[y : y + 6]
+            rows_ref[pl.ds(home(y + 6, 1) + x, 2, stride=3 * span), 0 : 2 * levels] = value[y + 6 : y + 8]
     for y in range(cy):
-        rows_ref[pl.ds(y * span + place[1], cx), 2 * levels :] = jnp.concatenate(
-            [cy_ref[y], cy_ref[y + 1]], axis=1
-        )
+        rows_ref[pl.ds(home(y, 1), cx), 2 * levels :] = jnp.concatenate([cy_ref[y], cy_ref[y + 1]], axis=1)
 
     area = area_ref[...]
     ey = ey_ref[...].T
@@ -68,19 +75,25 @@
     metric = []
     for length in (ex_ref[:, 0:cx], ex_ref[:, 1 : cx + 1], ey[0:cy], ey[1 : cy + 1]):
         metric += [length / area, gap]
-    metric = pltpu.roll(jnp.concatenate(metric, axis=1), place[2], 1)
+    metric = jnp.concatenate(metric, axis=1)
     lane_id = lax.broadcasted_iota(jnp.int32, (levels, lanes), 1)
-    here = (lane_id & (span - 1)) >> (cx.bit_length() - 1) == place[2] >> (cx.bit_length() - 1)
-
-    for first in range(0, cy, group):
-        block = rows_ref[first * span : (first + group) * span].T
-        for i in range(group):
-            y = first + i
+    first_lane = (lane_id & (span - 1)) & ~(cx - 1)
+    metrics = [(first_lane == place[j], pltpu.roll(metric, place[j], 1)) for j in (2, 3)]
+
+    for first in range(0, count, 3):
+        block = rows_ref[first * span : (first + 3) * span].T
+        for i in range(3):
+            r = first + i
             row = jnp.concatenate(
                 [block[q * levels : (q + 1) * levels, i * span : (i + 1) * span] for q in range(PARTS)],
                 axis=1,
             )
-            send_ref[pl.ds(y, levels, stride=cy), :] = jnp.where(here, metric[y : y + 1], row)
+            y = r // 6 * 8 + r % 6
+            row = jnp.where(metrics[0][0], metrics[0][1][y : y + 1], row)
+            if i == 2:
+                y = r // 6 * 8 + 6 + r % 6 // 3
+                row = jnp.where(metrics[1][0], metrics[1][1][y : y + 1], row)
+            send_ref[pl.ds(r, levels, stride=count), :] = row
 
 
 def unpack_kernel(recv_ref, out_ref):
@@ -159,10 +172,10 @@
     faces, side, lanes = field.shape
     cy, cx = side // tiles_high, side // tiles_wide
     slots = prod.shape[0]
-    slot_lanes = recv_ref.shape[2]
+    slot_lanes = recv_ref.shape[1]
     group = slot_lanes // (PARTS * cx)
     span = group * cx
-    lane_id = lax.broadcasted_iota(jnp.int32, (cy, slot_lanes), 1)
+    lane_id = lax.broadcasted_iota(jnp.int32, (8, slot_lanes), 1)
     place_id = (lane_id >> (cx.bit_length() - 1)) & (group - 1)
 
     def row_block(i):
@@ -170,34 +183,49 @@
         start = ty * cy
         return f, pl.ds(start if isinstance(i, int) else pl.multiple_of(start, 8), cy)
 
+    count_in = cy * 3 // 4
+
+    def spread(tiles):
+        blocks = []
+        for j in range(4):
+            block = tiles[0]
+            for tx in range(1, group):
+                block = jnp.where(place_id[0:6] == (tx + j) % group, tiles[tx], block)
+            if j:
+                ahead = pltpu.roll(block, slot_lanes - j * cx, 1)
+                around = pltpu.roll(block, span - j * cx, 1)
+                block = jnp.where(place_id[0:6] < group - j, ahead, around)
+            blocks.append(block)
+        last = blocks[3]
+        return [
+            jnp.concatenate([blocks[j], last[j : j + 1], last[3 + j : 4 + j]], axis=0) for j in range(3)
+        ]
+
     def assemble(i):
         f, rows = row_block(i)
-        values = []
-        for j in range(3):
-            blocks = []
+        for part in range(cy // 8):
+            groups = []
             for first in range(0, tiles_wide, group):
-                tiles = [recv_ref[i * tiles_wide + first + tx] for tx in range(group)]
-                block = tiles[0]
-                for tx in range(1, group):
-                    block = jnp.where(place_id == (tx + j) % group, tiles[tx], block)
-                if j:
-                    ahead = pltpu.roll(block, slot_lanes - j * cx, 1)
-                    around = pltpu.roll(block, span - j * cx, 1)
-                    block = jnp.where(place_id < group - j, ahead, around)
-                blocks.append(block)
-            if len(blocks) == 1:
-                values.append(blocks[0])
-            else:
+                start = (i * tiles_wide + first) * count_in + part * 6
+                groups.append(spread([recv_ref[pl.ds(start + tx * count_in, 6), :] for tx in range(group)]))
+            values = []
+            for blocks in zip(*groups):
+                if len(blocks) == 1:
+                    values.append(blocks[0])
+                    continue
                 values.append(
                     jnp.concatenate(
                         [block[:, q * span : (q + 1) * span] for q in range(PARTS) for block in blocks],
                         axis=1,
                     )
                 )
-        cells, courant, metric = values
-        field[f, rows, :] = cells
-        coef[0, f, rows, :] = courant
-        coef[1, f, rows, :] = courant * metric
+            cells, courant, metric = values
+            here = pl.ds(i // faces * cy + part * 8, 8)
+            if not isinstance(i, int):
+                here = pl.ds(pl.multiple_of(i // faces * cy + part * 8, 8), 8)
+            field[f, here, :] = cells
+            coef[0, f, here, :] = courant
+            coef[1, f, here, :] = courant * metric
 
     loop(faces * tiles_high, assemble)
 
@@ -230,6 +258,8 @@
     loop(faces, coefficients_y)
     prod[...] = jnp.zeros_like(prod)
     rim[...] = jnp.zeros_like(rim)
+    part_id = lax.broadcasted_iota(jnp.int32, (side, lanes), 1) >> (side.bit_length() - 1)
+    edge_id = lax.broadcasted_iota(jnp.int32, (8, lanes), 0)
     mirror_id = lax.broadcasted_iota(jnp.int32, (8, 128), 1)
     mirror_id = mirror_id ^ (side - 1)
     upside_id = 7 - lax.broadcasted_iota(jnp.int32, (8, 128), 0)
@@ -244,6 +274,22 @@
         return by_lanes(lambda chunk: jnp.take_along_axis(chunk, upside_id, axis=0), value)
 
     def sweep(d, between=None):
+        def overflow(f):
+            for low in range(2):
+                edge_rows = slice(0, 8) if low else slice(side - 8, side)
+                cells = field[f, edge_rows, :]
+                rows = None
+                for shift in (1, 2, 3):
+                    value = beta[d, 3 - shift if low else 3 + shift, f, edge_rows, :] * cells
+                    value = pltpu.roll(value, 8 - shift if low else shift, 0)
+                    value = jnp.where(edge_id >= 8 - shift if low else edge_id < shift, value, 0.0)
+                    rows = value if rows is None else rows + value
+                orders = (rows, upside(rows))
+                for order in range(2):
+                    value = orders[order ^ low]
+                    rim[0, order, f, low] = value
+                    rim[1, order, f, low] = mirrored(value)
+
         def apply(f):
             cells = field[f]
             here = prod.at[f % slots]
@@ -251,24 +297,11 @@
             for k in range(7):
                 if k != 3:
                     here[k, PAD : PAD + side, :] = beta[d, k, f] * cells
-            before, after = None, None
             for k in (0, 1, 2, 4, 5, 6):
-                shift = k - 3
-                middle = middle + here[k, PAD - shift : PAD - shift + side, :]
-                if shift < 0:
-                    term = here[k, PAD - 8 - shift : PAD - shift, :]
-                    before = term if before is None else before + term
-                else:
-                    term = here[k, PAD + side - shift : PAD + side + 8 - shift, :]
-                    after = term if after is None else after + term
+                middle = middle + here[k, PAD + 3 - k : PAD + 3 - k + side, :]
             acc[f] = middle
-            for low, rows in ((0, after), (1, before)):
-                orders = (rows, upside(rows))
-                for order in range(2):
-                    value = orders[order ^ low]
-                    rim[0, order, f, low] = value
-                    rim[1, order, f, low] = mirrored(value)
-
+
+        loop(faces, overflow)
         loop(faces, apply)
         if between:
             between()
@@ -289,9 +322,16 @@
             )
 
         def merge(group_faces):
-            blocks = turned_parts([with_seams(acc[f], f, d) for f in group_faces])
-            for f, parts in zip(group_faces, blocks):
-                field[f] = with_seams(jnp.concatenate(parts, axis=1), f, 1 - d)
+            for f in group_faces:
+                block = with_seams(acc[f], f, d)
+                if lanes == 128:
+                    pieces = split_parts(jnp.concatenate([block] * PARTS, axis=0).T, side, 0)
+                    block = pieces[0]
+                    for q in range(1, PARTS):
+                        block = jnp.where(part_id == q, pieces[q], block)
+                else:
+                    block = turned(block, side)
+                field[f] = with_seams(block, f, 1 - d)
 
         over_groups(merge)
 
@@ -306,17 +346,16 @@
 
     half = 8 // group
     row_id = lax.broadcasted_iota(jnp.int32, (8, slot_lanes), 0) >> (half.bit_length() - 1)
-    place = place_id[0:8]
+    place = place_id
 
     def tiles_to_rows(block):
-        bit = 1
-        while bit < group:
-            down = pltpu.roll(pltpu.roll(block, 8 - half * bit, 0), bit * cx, 1)
-            up = pltpu.roll(pltpu.roll(block, half * bit, 0), slot_lanes - bit * cx, 1)
-            a, b = row_id & bit, place & bit
-            block = jnp.where(a == b, block, jnp.where(a == 0, down, up))
-            bit *= 2
-        return block
+        value = block
+        for delta in range(1 - group, group):
+            if delta:
+                piece = pltpu.roll(block, -half * delta % 8, 0)
+                piece = pltpu.roll(piece, delta * cx % slot_lanes, 1)
+                value = jnp.where(place - row_id == delta, piece, value)
+        return value
 
     count = cy // group
 
@@ -379,10 +418,11 @@
         jnp.swapaxes(edge_y[0], 0, 1),
         cell_area[0],
     )
-    pack_rows = (cy * group * cx, lanes)
+    count_in = cy * 3 // 4
+    pack_rows = (count_in * group * cx, lanes)
     send = pl.pallas_call(
         pack_kernel,
-        out_shape=jax.ShapeDtypeStruct((levels * cy, slot), f32),
+        out_shape=jax.ShapeDtypeStruct((levels * count_in, slot), f32),
         in_specs=[HBM] * 6,
         out_specs=VMEM,
         scratch_shapes=[
@@ -395,7 +435,8 @@
     )(*map(in_hbm, arguments))
     if devices > levels:
         send = jnp.tile(send, (devices // levels, 1))
-    spheres = lax.all_to_all(send.reshape(devices, cy, slot), AXES, 0, 0, tiled=True)
+    pairs = send.reshape(devices * count_in // 2, 2, slot)
+    spheres = lax.all_to_all(pairs, AXES, 0, 0, tiled=True).reshape(devices * count_in, slot)
     scratch = [
         (2, 7, faces, side, width),
         (2, faces, side, width),
@@ -416,7 +457,7 @@
             pltpu.SMEM(seam_flip.shape, jnp.int32),
             pltpu.SemaphoreType.DMA((2,)),
         ],
-        compiler_params=grant((devices, cy, slot), back, *scratch),
+        compiler_params=grant(spheres.shape, back, *scratch),
         name="sphere",
     )(in_hbm(seam_partner), in_hbm(seam_flip), spheres)
     strips = lax.all_to_all(result, AXES, 0, 0, tiled=True)[: levels * cy // group]

time: 28.6 us -> 27.6 us (0.965)
  blocking collectives: 24.2 us -> 23.6 us
  Pallas kernels: 4.15 us -> 3.72 us
    all_to_all x1, blocking collectives: 9.23 us -> 8.88 us  [on_device(): lax.all_to_all(result, AXES, 0, 0, tiled=True)[:levels * cy // group]]
    pallas_call x1, Pallas kernels: 1.87 us -> 1.52 us  [on_device(): pl.pallas_call(functools.partial(sphere_kernel, tiles_high, tiles_wide),...]
where the time goes in v7:
time: 27.6 us; the launch traced here: 27.3 us
  blocking collectives  23.6 us (86%)
  Pallas kernels  3.72 us (13%)
    all_to_all x1, blocking collectives, on_device(): lax.all_to_all(pairs, AXES, 0, 0, tiled=True)  14.7 us
    all_to_all x1, blocking collectives, on_device(): lax.all_to_all(result, AXES, 0, 0, tiled=True)[:levels * cy // group]  8.88 us
    pallas_call x1, Pallas kernels, on_device(): pl.pallas_call(functools.partial(sphere_kernel, tiles_high, tiles_wide),...  1.52 us
    pallas_call x1, Pallas kernels, on_device(): pl.pallas_call(pack_kernel, out_shape=jax.ShapeDtypeStruct((levels * coun...  1.41 us
    pallas_call x1, Pallas kernels, on_device(): pl.pallas_call(unpack_kernel, out_shape=jax.ShapeDtypeStruct(cells.shape,...  0.79 us

profile of v7, /device:TPU:0, one launch (start us, length us, event | category | flops | bytes accessed | tf_op | source)
XLA Modules:
  0.0 27.3 jit_solution(1939567736562875767)
XLA Ops:
  0.0 1.4 %pack.1 = f32[192,128]{1,0:T(8,128)S(1)} custom-call(f32[8,8,128]{2,1,0:T(8,128)} %bitcast.21, f32[9,8,32]{2,1,0:T(8,128)} %bitcast.19, f32[8,9]{1,0:T(8,128)} %bitcast.22, f32[9,8,32]{2,1,0:T(8,128)} %bitcast.20, f32[8,9]{1,0:T(8,128)} %bitcast.23, f32[8,8]{1,0:T(8,128)} %bitcast.24), custom_call_target="tpu_custom_call" | custom-call | tf_op jit(solution)/shard_map/pack/pallas_call | solution.py:423
  1.4 14.7 %all_to_all.16 = f32[96,2,128]{2,1,0:T(2,128)S(1)} all-to-all(f32[96,2,128]{2,1,0:T(2,128)S(1)} %bitcast.16), channel_id=1, replica_groups=mesh['face'=2,'ty'=4,'tx'=4] {'ty','face','tx'}, dimensions={0} | all-to-all | bytes 196608 | tf_op jit(solution)/shard_map/all_to_all | solution.py:439
  16.1 1.5 %sphere.1 = f32[64,128]{1,0:T(8,128)S(1)} custom-call(s32[2,4]{1,0:T(2,128)} %partner_hbm.1, s32[2,4]{1,0:T(2,128)} %flip_hbm.1, f32[192,128]{1,0:T(8,128)S(1)} %bitcast.15), custom_call_target="tpu_custom_call" | custom-call | tf_op jit(solution)/shard_map/sphere/pallas_call | solution.py:449
  17.7 8.9 %all_to_all.17 = f32[32,2,128]{2,1,0:T(2,128)S(1)} all-to-all(f32[32,2,128]{2,1,0:T(2,128)S(1)} %bitcast.18), channel_id=1, replica_groups=mesh['face'=2,'ty'=4,'tx'=4] {'ty','face','tx'}, dimensions={0} | all-to-all | bytes 65536 | tf_op jit(solution)/shard_map/all_to_all | solution.py:463
  26.6 0.8 %unpack.1 = f32[8,8,128]{2,1,0:T(8,128)} custom-call(f32[64,128]{1,0:T(8,128)S(1)} %bitcast.17), custom_call_target="tpu_custom_call" | custom-call | tf_op jit(solution)/shard_map/unpack/pallas_call | solution.py:464

commit v8 on v7

--- a/solution.py
+++ b/solution.py
@@ -28,8 +28,17 @@
     return [lax.slice_in_dim(block, q * width, (q + 1) * width, axis=axis) for q in range(PARTS)]
 
 
-def turned(block, rows):
-    return jnp.concatenate(split_parts(block.T, rows, 0), axis=1)
+def turned_parts(block, rows):
+    if block.shape[0] * PARTS == 128:
+        return split_parts(jnp.concatenate([block] * PARTS, axis=0).T, rows, 0)
+    return [jnp.concatenate([part] * PARTS, axis=1) for part in split_parts(block.T, rows, 0)]
+
+
+def joined(parts, part_id):
+    value = parts[0]
+    for q in range(1, PARTS):
+        value = jnp.where(part_id == q, parts[q], value)
+    return value
 
 
 def pack_kernel(
@@ -60,14 +69,14 @@
         copy.start()
     for copy in copies:
         copy.wait()
-
-    for x in range(cx):
-        value = jnp.concatenate([cx_ref[x], cx_ref[x + 1]], axis=1)
+    along_x = [jnp.concatenate([cx_ref[x], cx_ref[x + 1]], axis=1) for x in range(cx)]
+    along_y = [jnp.concatenate([cy_ref[y], cy_ref[y + 1]], axis=1) for y in range(cy)]
+    for x, value in enumerate(along_x):
         for y in range(0, cy, 8):
             rows_ref[pl.ds(home(y, 1) + x, 6, stride=span), 0 : 2 * levels] = value[y : y + 6]
             rows_ref[pl.ds(home(y + 6, 1) + x, 2, stride=3 * span), 0 : 2 * levels] = value[y + 6 : y + 8]
-    for y in range(cy):
-        rows_ref[pl.ds(home(y, 1), cx), 2 * levels :] = jnp.concatenate([cy_ref[y], cy_ref[y + 1]], axis=1)
+    for y, value in enumerate(along_y):
+        rows_ref[pl.ds(home(y, 1), cx), 2 * levels :] = value
 
     area = area_ref[...]
     ey = ey_ref[...].T
@@ -80,20 +89,15 @@
     first_lane = (lane_id & (span - 1)) & ~(cx - 1)
     metrics = [(first_lane == place[j], pltpu.roll(metric, place[j], 1)) for j in (2, 3)]
 
-    for first in range(0, count, 3):
-        block = rows_ref[first * span : (first + 3) * span].T
-        for i in range(3):
-            r = first + i
-            row = jnp.concatenate(
-                [block[q * levels : (q + 1) * levels, i * span : (i + 1) * span] for q in range(PARTS)],
-                axis=1,
-            )
-            y = r // 6 * 8 + r % 6
-            row = jnp.where(metrics[0][0], metrics[0][1][y : y + 1], row)
-            if i == 2:
-                y = r // 6 * 8 + 6 + r % 6 // 3
-                row = jnp.where(metrics[1][0], metrics[1][1][y : y + 1], row)
-            send_ref[pl.ds(r, levels, stride=count), :] = row
+    part_id = lane_id >> (span.bit_length() - 1)
+    for r in range(count):
+        row = joined(turned_parts(rows_ref[r * span : (r + 1) * span], levels), part_id)
+        y = r // 6 * 8 + r % 6
+        row = jnp.where(metrics[0][0], metrics[0][1][y : y + 1], row)
+        if r % 3 == 2:
+            y = r // 6 * 8 + 6 + r % 6 // 3
+            row = jnp.where(metrics[1][0], metrics[1][1][y : y + 1], row)
+        send_ref[pl.ds(r, levels, stride=count), :] = row
 
 
 def unpack_kernel(recv_ref, out_ref):
@@ -102,16 +106,17 @@
     group = 128 // (PARTS * cx)
     half = 8 // group
     count = cy // group
+    part_id = lax.broadcasted_iota(jnp.int32, (cx, lanes), 1) >> (levels.bit_length() - 1)
     for r in range(count):
-        block = recv_ref[pl.ds(r, levels, stride=count), :].T
+        pieces = turned_parts(recv_ref[pl.ds(r, levels, stride=count), :], group * cx)
         for b in range(group):
-            out_ref[r // half * 8 + b * half + r % half] = jnp.concatenate(
-                [block[(q * group + b) * cx : (q * group + b + 1) * cx] for q in range(PARTS)], axis=1
+            out_ref[r // half * 8 + b * half + r % half] = joined(
+                [piece[b * cx : (b + 1) * cx] for piece in pieces], part_id
             )
 
 
 def stencil(*parts):
-    c_low, f_low, c_high, f_high = (jnp.concatenate([part] * PARTS, axis=1) for part in parts)
+    c_low, f_low, c_high, f_high = parts
 
     def interface(c, f):
         size = jnp.abs(c)
@@ -229,30 +234,17 @@
 
     loop(faces * tiles_high, assemble)
 
-    def over_groups(body):
-        if faces * side <= 128:
-            body(list(range(faces)))
-        else:
-            loop(faces, lambda f: body([f]))
-
-    def turned_parts(blocks):
-        if len(blocks) == 1:
-            return [split_parts(blocks[0].T, side, 0)]
-        block = jnp.concatenate(blocks, axis=0).T
-        return [
-            split_parts(block[:, i * side : (i + 1) * side], side, 0) for i in range(len(blocks))
-        ]
-
-    def coefficients_x(group_faces):
-        courant = turned_parts([coef[0, f] for f in group_faces])
-        scaled = turned_parts([coef[1, f] for f in group_faces])
-        for f, c, s in zip(group_faces, courant, scaled):
-            for k, value in enumerate(stencil(c[0], s[0], c[1], s[1])):
-                beta[0, k, f] = value
+    def coefficients_x(f):
+        c, s = turned_parts(coef[0, f], side), turned_parts(coef[1, f], side)
+        for k, value in enumerate(stencil(c[0], s[0], c[1], s[1])):
+            beta[0, k, f] = value
 
     def coefficients_y(f):
-        c, s = split_parts(coef[0, f], side, 1), split_parts(coef[1, f], side, 1)
-        for k, value in enumerate(stencil(c[2], s[2], c[3], s[3])):
+        c, s = (
+            [jnp.concatenate([part] * PARTS, axis=1) for part in split_parts(coef[i, f], side, 1)[2:]]
+            for i in range(2)
+        )
+        for k, value in enumerate(stencil(c[0], s[0], c[1], s[1])):
             beta[1, k, f] = value
 
     loop(faces, coefficients_y)
@@ -321,22 +313,14 @@
                 axis=0,
             )
 
-        def merge(group_faces):
-            for f in group_faces:
-                block = with_seams(acc[f], f, d)
-                if lanes == 128:
-                    pieces = split_parts(jnp.concatenate([block] * PARTS, axis=0).T, side, 0)
-                    block = pieces[0]
-                    for q in range(1, PARTS):
-                        block = jnp.where(part_id == q, pieces[q], block)
-                else:
-                    block = turned(block, side)
-                field[f] = with_seams(block, f, 1 - d)
-
-        over_groups(merge)
+        def merge(f):
+            block = joined(turned_parts(with_seams(acc[f], f, d), side), part_id)
+            field[f] = with_seams(block, f, 1 - d)
+
+        loop(faces, merge)
 
     def between():
-        over_groups(coefficients_x)
+        loop(faces, coefficients_x)
         for copy in copies:
             copy.wait()
 

time: 27.6 us -> 27.4 us (level)
  no operation moved by 1% of the time
where the time goes in v8:
time: 27.4 us; the launch traced here: 27.2 us
  blocking collectives  23.6 us (86%)
  Pallas kernels  3.55 us (13%)
    all_to_all x1, blocking collectives, on_device(): lax.all_to_all(pairs, AXES, 0, 0, tiled=True)  14.7 us
    all_to_all x1, blocking collectives, on_device(): lax.all_to_all(result, AXES, 0, 0, tiled=True)[:levels * cy // group]  8.88 us
    pallas_call x1, Pallas kernels, on_device(): pl.pallas_call(functools.partial(sphere_kernel, tiles_high, tiles_wide),...  1.52 us
    pallas_call x1, Pallas kernels, on_device(): pl.pallas_call(pack_kernel, out_shape=jax.ShapeDtypeStruct((levels * coun...  1.31 us
    pallas_call x1, Pallas kernels, on_device(): pl.pallas_call(unpack_kernel, out_shape=jax.ShapeDtypeStruct(cells.shape,...  0.71 us

profile of v8, /device:TPU:0, one launch (start us, length us, event | category | flops | bytes accessed | tf_op | source)
XLA Modules:
  0.0 27.2 jit_solution(2336948221109387905)
XLA Ops:
  0.0 1.3 %pack.1 = f32[192,128]{1,0:T(8,128)S(1)} custom-call(f32[8,8,128]{2,1,0:T(8,128)} %bitcast.21, f32[9,8,32]{2,1,0:T(8,128)} %bitcast.19, f32[8,9]{1,0:T(8,128)} %bitcast.22, f32[9,8,32]{2,1,0:T(8,128)} %bitcast.20, f32[8,9]{1,0:T(8,128)} %bitcast.23, f32[8,8]{1,0:T(8,128)} %bitcast.24), custom_call_target="tpu_custom_call" | custom-call | tf_op jit(solution)/shard_map/pack/pallas_call | solution.py:407
  1.3 14.7 %all_to_all.16 = f32[96,2,128]{2,1,0:T(2,128)S(1)} all-to-all(f32[96,2,128]{2,1,0:T(2,128)S(1)} %bitcast.16), channel_id=1, replica_groups=mesh['face'=2,'ty'=4,'tx'=4] {'ty','face','tx'}, dimensions={0} | all-to-all | bytes 196608 | tf_op jit(solution)/shard_map/all_to_all | solution.py:423
  16.0 1.5 %sphere.1 = f32[64,128]{1,0:T(8,128)S(1)} custom-call(s32[2,4]{1,0:T(2,128)} %partner_hbm.1, s32[2,4]{1,0:T(2,128)} %flip_hbm.1, f32[192,128]{1,0:T(8,128)S(1)} %bitcast.15), custom_call_target="tpu_custom_call" | custom-call | tf_op jit(solution)/shard_map/sphere/pallas_call | solution.py:433
  17.6 8.9 %all_to_all.17 = f32[32,2,128]{2,1,0:T(2,128)S(1)} all-to-all(f32[32,2,128]{2,1,0:T(2,128)S(1)} %bitcast.18), channel_id=1, replica_groups=mesh['face'=2,'ty'=4,'tx'=4] {'ty','face','tx'}, dimensions={0} | all-to-all | bytes 65536 | tf_op jit(solution)/shard_map/all_to_all | solution.py:447
  26.5 0.7 %unpack.1 = f32[8,8,128]{2,1,0:T(8,128)} custom-call(f32[64,128]{1,0:T(8,128)S(1)} %bitcast.17), custom_call_target="tpu_custom_call" | custom-call | tf_op jit(solution)/shard_map/unpack/pallas_call | solution.py:448

commit v9 on v8

--- a/solution.py
+++ b/solution.py
@@ -42,7 +42,24 @@
 
 
 def pack_kernel(
-    cot_hbm, cx_hbm, ex_hbm, cy_hbm, ey_hbm, area_hbm, send_ref, rows_ref, cx_ref, ex_ref, cy_ref, ey_ref, area_ref, sems
+    cot_hbm,
+    cx_hbm,
+    ex_hbm,
+    cy_hbm,
+    ey_hbm,
+    area_hbm,
+    partner_hbm,
+    flip_hbm,
+    send_ref,
+    partner_ref,
+    flip_ref,
+    rows_ref,
+    cx_ref,
+    ex_ref,
+    cy_ref,
+    ey_ref,
+    area_ref,
+    sems,
 ):
     cy, cx = area_ref.shape
     lanes = rows_ref.shape[1]
@@ -63,11 +80,12 @@
         for i, (source, target) in enumerate(
             [(ex_hbm, ex_ref), (ey_hbm, ey_ref), (area_hbm, area_ref), (cx_hbm, cx_ref), (cy_hbm, cy_ref)]
             + [(cot_hbm.at[y], rows_ref.at[pl.ds(home(y, 0), cx)]) for y in range(cy)]
+            + [(partner_hbm, partner_ref), (flip_hbm, flip_ref)]
         )
     ]
     for copy in copies:
         copy.start()
-    for copy in copies:
+    for copy in copies[:-2]:
         copy.wait()
     along_x = [jnp.concatenate([cx_ref[x], cx_ref[x + 1]], axis=1) for x in range(cx)]
     along_y = [jnp.concatenate([cy_ref[y], cy_ref[y + 1]], axis=1) for y in range(cy)]
@@ -78,7 +96,7 @@
     for y, value in enumerate(along_y):
         rows_ref[pl.ds(home(y, 1), cx), 2 * levels :] = value
 
-    area = area_ref[...]
+    area = 12.0 * area_ref[...]
     ey = ey_ref[...].T
     gap = jnp.zeros((cy, span - cx), jnp.float32)
     metric = []
@@ -98,6 +116,8 @@
             y = r // 6 * 8 + 6 + r % 6 // 3
             row = jnp.where(metrics[1][0], metrics[1][1][y : y + 1], row)
         send_ref[pl.ds(r, levels, stride=count), :] = row
+    for copy in copies[-2:]:
+        copy.wait()
 
 
 def unpack_kernel(recv_ref, out_ref):
@@ -120,23 +140,23 @@
 
     def interface(c, f):
         size = jnp.abs(c)
-        half = 0.5 * size
-        w = 3.0 * half * (1.0 - (2.0 / 3.0) * size)
+        rest = 1.0 - size
+        part = f * size
+        centre = f * rest * rest
+        outer = part * rest
+        cell = part * (12.0 + 24.0 * rest)
+        middle = 7.0 * centre
+        cell = cell - 7.0 * outer
         plus = c > 0
-        centre = f * (1.0 - half - w)
-        outer = f * (half - w)
-        cell = f * (2.0 * w)
-        zero = jnp.zeros_like(c)
-        o_low, o_high = jnp.where(plus, outer, zero), jnp.where(plus, zero, outer)
-        s_low, s_high = jnp.where(plus, cell, zero), jnp.where(plus, zero, cell)
-        near, far = 7.0 / 12.0, 1.0 / 12.0
+        first = jnp.where(plus, outer, 0.0)
+        last = outer - first
         return (
-            -far * o_low,
-            near * o_low - far * centre,
-            near * (centre + o_low) - far * o_high + s_low,
-            near * (centre + o_high) - far * o_low + s_high,
-            near * o_high - far * centre,
-            -far * o_high,
+            first,
+            -7.0 * first - centre,
+            middle + jnp.where(plus, cell, outer),
+            middle + jnp.where(plus, outer, cell),
+            -7.0 * last - centre,
+            last,
         )
 
     low, high = interface(c_low, f_low), interface(c_high, f_high)
@@ -154,8 +174,8 @@
 def sphere_kernel(
     tiles_high,
     tiles_wide,
-    partner_hbm,
-    flip_hbm,
+    partner_vmem,
+    flip_vmem,
     recv_ref,
     out_ref,
     beta,
@@ -169,8 +189,8 @@
     sems,
 ):
     copies = [
-        pltpu.make_async_copy(partner_hbm, partner_ref, sems.at[0]),
-        pltpu.make_async_copy(flip_hbm, flip_ref, sems.at[1]),
+        pltpu.make_async_copy(partner_vmem, partner_ref, sems.at[0]),
+        pltpu.make_async_copy(flip_vmem, flip_ref, sems.at[1]),
     ]
     for copy in copies:
         copy.start()
@@ -401,18 +421,24 @@
         courant_y[0],
         jnp.swapaxes(edge_y[0], 0, 1),
         cell_area[0],
+        seam_partner,
+        seam_flip,
     )
     count_in = cy * 3 // 4
     pack_rows = (count_in * group * cx, lanes)
-    send = pl.pallas_call(
+    send, partner, flip = pl.pallas_call(
         pack_kernel,
-        out_shape=jax.ShapeDtypeStruct((levels * count_in, slot), f32),
-        in_specs=[HBM] * 6,
-        out_specs=VMEM,
+        out_shape=(
+            jax.ShapeDtypeStruct((levels * count_in, slot), f32),
+            jax.ShapeDtypeStruct(seam_partner.shape, jnp.int32),
+            jax.ShapeDtypeStruct(seam_flip.shape, jnp.int32),
+        ),
+        in_specs=[HBM] * 8,
+        out_specs=(VMEM, VMEM, VMEM),
         scratch_shapes=[
             pltpu.VMEM(pack_rows, f32),
-            *[pltpu.VMEM(argument.shape, f32) for argument in arguments[1:]],
-            pltpu.SemaphoreType.DMA((5 + cy,)),
+            *[pltpu.VMEM(argument.shape, f32) for argument in arguments[1:6]],
+            pltpu.SemaphoreType.DMA((7 + cy,)),
         ],
         compiler_params=grant(*[cells.shape] * 4, pack_rows, (levels, cy, slot)),
         name="pack",
@@ -433,7 +459,7 @@
     result = pl.pallas_call(
         functools.partial(sphere_kernel, tiles_high, tiles_wide),
         out_shape=jax.ShapeDtypeStruct(back, f32),
-        in_specs=[HBM, HBM, VMEM],
+        in_specs=[VMEM, VMEM, VMEM],
         out_specs=VMEM,
         scratch_shapes=[
             *[pltpu.VMEM(shape, f32) for shape in scratch],
@@ -443,7 +469,7 @@
         ],
         compiler_params=grant(spheres.shape, back, *scratch),
         name="sphere",
-    )(in_hbm(seam_partner), in_hbm(seam_flip), spheres)
+    )(partner, flip, spheres)
     strips = lax.all_to_all(result, AXES, 0, 0, tiled=True)[: levels * cy // group]
     return pl.pallas_call(
         unpack_kernel,

time: 27.4 us -> 27.3 us (level)
  no operation moved by 1% of the time
where the time goes in v9:
time: 27.3 us; the launch traced here: 27 us
  blocking collectives  23.6 us (86%)
  Pallas kernels  3.42 us (13%)
    all_to_all x1, blocking collectives, on_device(): lax.all_to_all(pairs, AXES, 0, 0, tiled=True)  14.7 us
    all_to_all x1, blocking collectives, on_device(): lax.all_to_all(result, AXES, 0, 0, tiled=True)[:levels * cy // group]  8.88 us
    pallas_call x1, Pallas kernels, on_device(): pl.pallas_call(functools.partial(sphere_kernel, tiles_high, tiles_wide),...  1.37 us
    pallas_call x1, Pallas kernels, on_device(): pl.pallas_call(pack_kernel, out_shape=(jax.ShapeDtypeStruct((levels * cou...  1.34 us
    pallas_call x1, Pallas kernels, on_device(): pl.pallas_call(unpack_kernel, out_shape=jax.ShapeDtypeStruct(cells.shape,...  0.71 us

profile of v9, /device:TPU:0, one launch (start us, length us, event | category | flops | bytes accessed | tf_op | source)
XLA Modules:
  0.0 27.0 jit_solution(6990960371171009526)
XLA Ops:
  0.0 1.3 %pack.1 = (f32[192,128]{1,0:T(8,128)S(1)}, s32[2,4]{1,0:T(2,128)S(1)}, s32[2,4]{1,0:T(2,128)S(1)}) custom-call(f32[8,8,128]{2,1,0:T(8,128)} %bitcast.21, f32[9,8,32]{2,1,0:T(8,128)} %bitcast.19, f32[8,9]{1,0:T(8,128)} %bitcast.22, f32[9,8,32]{2,1,0:T(8,128)} %bitcast.20, f32[8,9]{1,0:T(8,128)} %bitcast.23, f32[8,8]{1,0:T(8,128)} %bitcast.24, ...), custom_call_target="tpu_custom_call" | custom-call | tf_op jit(solution)/shard_map/pack/pallas_call | solution.py:429
  1.3 14.7 %all_to_all.16 = f32[96,2,128]{2,1,0:T(2,128)S(1)} all-to-all(f32[96,2,128]{2,1,0:T(2,128)S(1)} %bitcast.18), channel_id=1, replica_groups=mesh['face'=2,'ty'=4,'tx'=4] {'ty','face','tx'}, dimensions={0} | all-to-all | bytes 196608 | tf_op jit(solution)/shard_map/all_to_all | solution.py:449
  16.1 1.4 %sphere.1 = f32[64,128]{1,0:T(8,128)S(1)} custom-call(s32[2,4]{1,0:T(2,128)S(1)} %get-tuple-element.8.partner_vmem, s32[2,4]{1,0:T(2,128)S(1)} %get-tuple-element.9.flip_vmem, f32[192,128]{1,0:T(8,128)S(1)} %bitcast.15), custom_call_target="tpu_custom_call" | custom-call | tf_op jit(solution)/shard_map/sphere/pallas_call | solution.py:459
  17.4 8.9 %all_to_all.17 = f32[32,2,128]{2,1,0:T(2,128)S(1)} all-to-all(f32[32,2,128]{2,1,0:T(2,128)S(1)} %bitcast.17), channel_id=1, replica_groups=mesh['face'=2,'ty'=4,'tx'=4] {'ty','face','tx'}, dimensions={0} | all-to-all | bytes 65536 | tf_op jit(solution)/shard_map/all_to_all | solution.py:473
  26.3 0.7 %unpack.1 = f32[8,8,128]{2,1,0:T(8,128)} custom-call(f32[64,128]{1,0:T(8,128)S(1)} %bitcast.16), custom_call_target="tpu_custom_call" | custom-call | tf_op jit(solution)/shard_map/unpack/pallas_call | solution.py:474

commit v10 on v9

--- a/solution.py
+++ b/solution.py
@@ -54,6 +54,7 @@
     partner_ref,
     flip_ref,
     rows_ref,
+    cot_ref,
     cx_ref,
     ex_ref,
     cy_ref,
@@ -78,8 +79,8 @@
     copies = [
         pltpu.make_async_copy(source, target, sems.at[i])
         for i, (source, target) in enumerate(
-            [(ex_hbm, ex_ref), (ey_hbm, ey_ref), (area_hbm, area_ref), (cx_hbm, cx_ref), (cy_hbm, cy_ref)]
-            + [(cot_hbm.at[y], rows_ref.at[pl.ds(home(y, 0), cx)]) for y in range(cy)]
+            [(cx_hbm, cx_ref), (cy_hbm, cy_ref), (cot_hbm, cot_ref), (ex_hbm, ex_ref), (ey_hbm, ey_ref)]
+            + [(area_hbm, area_ref)]
             + [(partner_hbm, partner_ref), (flip_hbm, flip_ref)]
         )
     ]
@@ -87,6 +88,8 @@
         copy.start()
     for copy in copies[:-2]:
         copy.wait()
+    for y in range(cy):
+        rows_ref[pl.ds(home(y, 0), cx), :] = cot_ref[y]
     along_x = [jnp.concatenate([cx_ref[x], cx_ref[x + 1]], axis=1) for x in range(cx)]
     along_y = [jnp.concatenate([cy_ref[y], cy_ref[y + 1]], axis=1) for y in range(cy)]
     for x, value in enumerate(along_x):
@@ -268,8 +271,8 @@
             beta[1, k, f] = value
 
     loop(faces, coefficients_y)
-    prod[...] = jnp.zeros_like(prod)
-    rim[...] = jnp.zeros_like(rim)
+    for start in (PAD - 8, PAD + side):
+        prod[:, :, start : start + 8, :] = jnp.zeros((slots, 7, 8, lanes), jnp.float32)
     part_id = lax.broadcasted_iota(jnp.int32, (side, lanes), 1) >> (side.bit_length() - 1)
     edge_id = lax.broadcasted_iota(jnp.int32, (8, lanes), 0)
     mirror_id = lax.broadcasted_iota(jnp.int32, (8, 128), 1)
@@ -437,8 +440,8 @@
         out_specs=(VMEM, VMEM, VMEM),
         scratch_shapes=[
             pltpu.VMEM(pack_rows, f32),
-            *[pltpu.VMEM(argument.shape, f32) for argument in arguments[1:6]],
-            pltpu.SemaphoreType.DMA((7 + cy,)),
+            *[pltpu.VMEM(argument.shape, f32) for argument in arguments[:6]],
+            pltpu.SemaphoreType.DMA((8,)),
         ],
         compiler_params=grant(*[cells.shape] * 4, pack_rows, (levels, cy, slot)),
         name="pack",

time: 27.3 us -> 27.1 us (level)
  no operation moved by 1% of the time
where the time goes in v10:
time: 27.1 us; the launch traced here: 26.9 us
  blocking collectives  23.6 us (87%)
  Pallas kernels  3.31 us (12%)
    all_to_all x1, blocking collectives, on_device(): lax.all_to_all(pairs, AXES, 0, 0, tiled=True)  14.7 us
    all_to_all x1, blocking collectives, on_device(): lax.all_to_all(result, AXES, 0, 0, tiled=True)[:levels * cy // group]  8.88 us
    pallas_call x1, Pallas kernels, on_device(): pl.pallas_call(functools.partial(sphere_kernel, tiles_high, tiles_wide),...  1.37 us
    pallas_call x1, Pallas kernels, on_device(): pl.pallas_call(pack_kernel, out_shape=(jax.ShapeDtypeStruct((levels * cou...  1.22 us
    pallas_call x1, Pallas kernels, on_device(): pl.pallas_call(unpack_kernel, out_shape=jax.ShapeDtypeStruct(cells.shape,...  0.71 us

profile of v10, /device:TPU:0, one launch (start us, length us, event | category | flops | bytes accessed | tf_op | source)
XLA Modules:
  0.0 26.9 jit_solution(1065966259687981801)
XLA Ops:
  0.0 1.2 %pack.1 = (f32[192,128]{1,0:T(8,128)S(1)}, s32[2,4]{1,0:T(2,128)S(1)}, s32[2,4]{1,0:T(2,128)S(1)}) custom-call(f32[8,8,128]{2,1,0:T(8,128)} %bitcast.21, f32[9,8,32]{2,1,0:T(8,128)} %bitcast.19, f32[8,9]{1,0:T(8,128)} %bitcast.22, f32[9,8,32]{2,1,0:T(8,128)} %bitcast.20, f32[8,9]{1,0:T(8,128)} %bitcast.23, f32[8,8]{1,0:T(8,128)} %bitcast.24, ...), custom_call_target="tpu_custom_call" | custom-call | tf_op jit(solution)/shard_map/pack/pallas_call | solution.py:432
  1.2 14.7 %all_to_all.16 = f32[96,2,128]{2,1,0:T(2,128)S(1)} all-to-all(f32[96,2,128]{2,1,0:T(2,128)S(1)} %bitcast.18), channel_id=1, replica_groups=mesh['face'=2,'ty'=4,'tx'=4] {'ty','face','tx'}, dimensions={0} | all-to-all | bytes 196608 | tf_op jit(solution)/shard_map/all_to_all | solution.py:452
  16.0 1.4 %sphere.1 = f32[64,128]{1,0:T(8,128)S(1)} custom-call(s32[2,4]{1,0:T(2,128)S(1)} %get-tuple-element.8.partner_vmem, s32[2,4]{1,0:T(2,128)S(1)} %get-tuple-element.9.flip_vmem, f32[192,128]{1,0:T(8,128)S(1)} %bitcast.15), custom_call_target="tpu_custom_call" | custom-call | tf_op jit(solution)/shard_map/sphere/pallas_call | solution.py:462
  17.3 8.9 %all_to_all.17 = f32[32,2,128]{2,1,0:T(2,128)S(1)} all-to-all(f32[32,2,128]{2,1,0:T(2,128)S(1)} %bitcast.17), channel_id=1, replica_groups=mesh['face'=2,'ty'=4,'tx'=4] {'ty','face','tx'}, dimensions={0} | all-to-all | bytes 65536 | tf_op jit(solution)/shard_map/all_to_all | solution.py:476
  26.2 0.7 %unpack.1 = f32[8,8,128]{2,1,0:T(8,128)} custom-call(f32[64,128]{1,0:T(8,128)S(1)} %bitcast.16), custom_call_target="tpu_custom_call" | custom-call | tf_op jit(solution)/shard_map/unpack/pallas_call | solution.py:477

commit v11 on v10

--- a/solution.py
+++ b/solution.py
@@ -336,11 +336,17 @@
                 axis=0,
             )
 
-        def merge(f):
-            block = joined(turned_parts(with_seams(acc[f], f, d), side), part_id)
-            field[f] = with_seams(block, f, 1 - d)
-
-        loop(faces, merge)
+        if lanes == 128:
+            blocks = [turned_parts(with_seams(acc[f], f, d), side) for f in range(faces)]
+            for f in range(faces):
+                field[f] = with_seams(joined(blocks[f], part_id), f, 1 - d)
+        else:
+
+            def merge(f):
+                block = joined(turned_parts(with_seams(acc[f], f, d), side), part_id)
+                field[f] = with_seams(block, f, 1 - d)
+
+            loop(faces, merge)
 
     def between():
         loop(faces, coefficients_x)

time: 27.1 us -> 27.1 us (level)
  no operation moved by 1% of the time
where the time goes in v11:
time: 27.1 us; the launch traced here: 26.9 us
  blocking collectives  23.6 us (87%)
  Pallas kernels  3.31 us (12%)
    all_to_all x1, blocking collectives, on_device(): lax.all_to_all(pairs, AXES, 0, 0, tiled=True)  14.7 us
    all_to_all x1, blocking collectives, on_device(): lax.all_to_all(result, AXES, 0, 0, tiled=True)[:levels * cy // group]  8.88 us
    pallas_call x1, Pallas kernels, on_device(): pl.pallas_call(functools.partial(sphere_kernel, tiles_high, tiles_wide),...  1.37 us
    pallas_call x1, Pallas kernels, on_device(): pl.pallas_call(pack_kernel, out_shape=(jax.ShapeDtypeStruct((levels * cou...  1.22 us
    pallas_call x1, Pallas kernels, on_device(): pl.pallas_call(unpack_kernel, out_shape=jax.ShapeDtypeStruct(cells.shape,...  0.71 us

profile of v11, /device:TPU:0, one launch (start us, length us, event | category | flops | bytes accessed | tf_op | source)
XLA Modules:
  0.0 26.9 jit_solution(1065966259687981801)
XLA Ops:
  0.0 1.2 %pack.1 = (f32[192,128]{1,0:T(8,128)S(1)}, s32[2,4]{1,0:T(2,128)S(1)}, s32[2,4]{1,0:T(2,128)S(1)}) custom-call(f32[8,8,128]{2,1,0:T(8,128)} %bitcast.21, f32[9,8,32]{2,1,0:T(8,128)} %bitcast.19, f32[8,9]{1,0:T(8,128)} %bitcast.22, f32[9,8,32]{2,1,0:T(8,128)} %bitcast.20, f32[8,9]{1,0:T(8,128)} %bitcast.23, f32[8,8]{1,0:T(8,128)} %bitcast.24, ...), custom_call_target="tpu_custom_call" | custom-call | tf_op jit(solution)/shard_map/pack/pallas_call | solution.py:438
  1.2 14.7 %all_to_all.16 = f32[96,2,128]{2,1,0:T(2,128)S(1)} all-to-all(f32[96,2,128]{2,1,0:T(2,128)S(1)} %bitcast.18), channel_id=1, replica_groups=mesh['face'=2,'ty'=4,'tx'=4] {'ty','face','tx'}, dimensions={0} | all-to-all | bytes 196608 | tf_op jit(solution)/shard_map/all_to_all | solution.py:458
  16.0 1.4 %sphere.1 = f32[64,128]{1,0:T(8,128)S(1)} custom-call(s32[2,4]{1,0:T(2,128)S(1)} %get-tuple-element.8.partner_vmem, s32[2,4]{1,0:T(2,128)S(1)} %get-tuple-element.9.flip_vmem, f32[192,128]{1,0:T(8,128)S(1)} %bitcast.15), custom_call_target="tpu_custom_call" | custom-call | tf_op jit(solution)/shard_map/sphere/pallas_call | solution.py:468
  17.3 8.9 %all_to_all.17 = f32[32,2,128]{2,1,0:T(2,128)S(1)} all-to-all(f32[32,2,128]{2,1,0:T(2,128)S(1)} %bitcast.17), channel_id=1, replica_groups=mesh['face'=2,'ty'=4,'tx'=4] {'ty','face','tx'}, dimensions={0} | all-to-all | bytes 65536 | tf_op jit(solution)/shard_map/all_to_all | solution.py:482
  26.2 0.7 %unpack.1 = f32[8,8,128]{2,1,0:T(8,128)} custom-call(f32[64,128]{1,0:T(8,128)S(1)} %bitcast.16), custom_call_target="tpu_custom_call" | custom-call | tf_op jit(solution)/shard_map/unpack/pallas_call | solution.py:483
